TPU v7x, 256 devices: a whole 4x4x8 slice. The times are simulated.
256 devices in a mesh: row: 16 (over z_lo, y), col: 16 (over z_hi, x, core).
Axes of the slice: x: 4, y: 4, z: 8 (z_hi: 2, z_lo: 4; z = z_hi * 4 + z_lo), core: 2. Of those that a mesh axis runs over, the one named last changes fastest.
Arguments:
- lambda_amps: float32 [256, 32768], P('col', 'row'), may hold values from -6 to 6
- cycle_inter: float32 [32768, 4096], P('row', 'col'), may hold values from -0.03125 to 0.03125
- exchanged: int32 [4096], replicated, may hold values from 0 to 4095, each once
- occ_energy: float32 [64], replicated, may hold values from -1 to -0.25
- virt_energy: float32 [512], replicated, may hold values from 0.25 to 1.5
- row_orbitals: int32 [256, 2], replicated, may hold values from 0 to 63
- col_orbitals: int32 [4096, 2], replicated, may hold values from 0 to 511
Outputs:
- update: float32 [256, 4096], P(('row', 'col'))
All inputs are finite; a program needn't handle non-finite values.
Results may differ from a plain program's by a relative error of at most 0.000088.
Values sent between devices are 32-bit elements; how exact they have to be, the bound alone decides.
No kernel may reach another device: no remote copies, remote signals or barrier semaphores. Data moves between devices by JAX's collectives and lax.ppermute only.
A program may use at most 64 MiB of HBM per device.

v0:
```python
import jax
import jax.numpy as jnp
from jax import lax
from jax.sharding import PartitionSpec as P


def shards(
    lambda_amps, cycle_inter, exchanged, occ_energy, virt_energy, row_orbitals, col_orbitals
):
    n_row = lax.axis_size("row")
    n_col = lax.axis_size("col")
    per_owner = lambda_amps.shape[0] // n_row
    partial_value = jnp.dot(
        lax.all_gather(lambda_amps, "col", axis=0, tiled=True),
        cycle_inter,
        precision=lax.Precision.HIGHEST,
        preferred_element_type=jnp.float32,
    )
    summed = lax.psum_scatter(partial_value, "row", scatter_dimension=0, tiled=True)
    cycle = lax.all_to_all(summed, "col", split_axis=0, concat_axis=1, tiled=True)
    anti = cycle - jnp.take(cycle, exchanged, axis=1)
    first_row = (lax.axis_index("row") * n_col + lax.axis_index("col")) * per_owner
    mine = lax.dynamic_slice_in_dim(row_orbitals, first_row, per_owner, 0)
    row_part = jnp.take(occ_energy, mine[:, 0]) + jnp.take(occ_energy, mine[:, 1])
    col_part = jnp.take(virt_energy, col_orbitals[:, 0]) + jnp.take(virt_energy, col_orbitals[:, 1])
    denom = row_part[:, None] - col_part[None, :]
    return anti / denom


def solution(mesh):
    placed = (P("col", "row"), P("row", "col"), P(), P(), P(), P(), P())
    return jax.shard_map(
        shards, mesh=mesh, in_specs=placed, out_specs=P(("row", "col"), None), check_vma=False
    )
```

profile of v0, /device:TPU:1, one launch (start us, length us, event | category | flops | bytes accessed | tf_op | source)
XLA Modules:
  0.0 258.8 jit_solution(6470950370297978976)
XLA Ops:
  6.5 0.0 copy-start
  6.5 0.0 all-gather.2.cloned.1.call-start
  6.5 0.7 all-gather.2.cloned.1.call-update
  7.3 0.0 reduce-scatter.2.cloned.1.call-start
  7.3 0.7 fusion.2
  8.0 0.9 fusion.5
  8.9 0.0 copy-start.4
  8.9 0.0 copy-start.1
  8.9 68.1 %all-gather.2.cloned.1.call-done = f32[256,2048]{1,0:T(8,128)} async-done(((f32[16,2048]{1,0:T(8,128)}), f32[256,2048]{1,0:T(8,128)}) %all-gather.2.cloned.1.call-update) | async-done | bytes 2097168 | tf_op jit(solution)/shard_map/all_gather | solution.py:14
  77.0 0.0 copy-done
  77.0 4.2 %fusion.8 = f32[256,256]{1,0:T(8,128)} fusion(f32[256,2048]{1,0:T(8,128)} %all-gather.2.cloned.1.call-done, f32[2048,256]{1,0:T(8,128)S(1)} %copy-done), kind=kOutput, calls=%fused_computation.16 | convolution fusion | flops 1610612736 | bytes 4456448 | tf_op jit(solution)/shard_map/dot_general | solution.py:13
  81.2 0.0 reduce-scatter.2.cloned.1.call-update
  81.2 0.0 copy-done.4
  81.2 0.1 constant_dynamic-slice_fusion
  81.3 67.7 %reduce-scatter.2.cloned.1.call-done = f32[16,256]{1,0:T(8,128)} async-done(((f32[256,256]{1,0:T(8,128)}), f32[16,256]{1,0:T(8,128)}) %reduce-scatter.2.cloned.1.call-update) | async-done | bytes 16400 | tf_op jit(solution)/shard_map/reduce_scatter | solution.py:19
  149.0 1.3 copy.8
  150.3 19.8 %all-to-all-start = ((f32[16,1,256]{2,1,0:T(1,128)}), f32[16,1,256]{2,1,0:T(1,128)S(1)}, u32[]{:S(2)}, u32[]{:S(2)}) async-start(f32[16,1,256]{2,1,0:T(1,128)} %copy.8), calls=%async_computation.1 | async-start | bytes 32768 | tf_op jit(solution)/shard_map/all_to_all | solution.py:20
  170.2 0.6 fusion.6
  174.5 0.0 copy-done.1
  174.5 25.9 %gather_fusion.2 = f32[4096]{0:T(1024)S(1)} fusion(f32[512]{0:T(512)S(1)} %copy-done.1, s32[4096]{0:T(1024)S(1)} %fusion.4), kind=kCustom, calls=%fused_computation.1.clone | custom fusion | bytes 49152 | tf_op jit(solution)/shard_map/jit(_take)/gather | solution.py:25
  200.4 0.0 copy-start.3
  200.4 25.9 %gather_fusion.1 = f32[4096]{0:T(1024)S(1)} fusion(f32[512]{0:T(512)S(1)} %copy-done.1, s32[4096]{0:T(1024)S(1)} %fusion.3), kind=kCustom, calls=%fused_computation.clone | custom fusion | bytes 49152 | tf_op jit(solution)/shard_map/jit(_take)/gather | solution.py:25
  226.3 0.0 copy-done.3
  226.4 0.7 fusion.7
  228.3 0.0 all-to-all-done
  228.3 0.0 copy-start.2
  228.3 23.0 %gather_fusion = f32[4096]{0:T(1024)S(1)} fusion(f32[4096]{0:T(1024)S(1)} %bitcast.12, s32[4096]{0:T(1024)S(1)} %fusion.2), kind=kCustom, calls=%fused_computation.2 | custom fusion | bytes 49152 | tf_op jit(solution)/shard_map/jit(_take)/gather | solution.py:21
  251.3 0.0 copy-done.2
  251.3 0.6 fusion.1
  (2 shorter events, 0.0 us)
Async XLA Ops:
  6.5 70.5 %copy-start = (f32[2048,256]{1,0:T(8,128)S(1)}, f32[2048,256]{1,0:T(8,128)}, u32[]{:S(2)}) copy-start(f32[2048,256]{1,0:T(8,128)} %param.10) | copy-start | bytes 6291460
  6.5 70.5 %all-gather.2.cloned.1.call-start = ((), (), s32[]{:S(2)}) async-start(), calls=%async_computation.2 | async-start | bytes 2228224 | tf_op jit(solution)/shard_map/all_gather | solution.py:14
  7.3 141.7 %reduce-scatter.2.cloned.1.call-start = ((), (), s32[]{:S(2)}) async-start(), calls=%async_computation.3 | async-start | bytes 278528 | tf_op jit(solution)/shard_map/reduce_scatter | solution.py:19
  8.9 72.3 %copy-start.4 = (s32[256,2]{0,1:T(2,128)S(1)}, s32[256,2]{0,1:T(2,128)}, u32[]{:S(2)}) copy-start(s32[256,2]{0,1:T(2,128)} %param.14) | copy-start | bytes 6148
  8.9 165.6 %copy-start.1 = (f32[512]{0:T(512)S(1)}, f32[512]{0:T(512)}, u32[]{:S(2)}) copy-start(f32[512]{0:T(512)} %param.13) | copy-start | bytes 6148
  150.3 77.9 %all-to-all-start = ((f32[16,1,256]{2,1,0:T(1,128)}), f32[16,1,256]{2,1,0:T(1,128)S(1)}, u32[]{:S(2)}, u32[]{:S(2)}) async-start(f32[16,1,256]{2,1,0:T(1,128)} %copy.8), calls=%async_computation.1 | async-start | bytes 32768 | tf_op jit(solution)/shard_map/all_to_all | solution.py:20
  200.4 25.9 %copy-start.3 = (f32[64]{0:T(128)S(1)}, f32[64]{0:T(128)}, u32[]{:S(2)}) copy-start(f32[64]{0:T(128)} %param.12) | copy-start | bytes 772
  228.3 23.1 %copy-start.2 = (s32[4096]{0:T(1024)S(1)}, s32[4096]{0:T(1024)}, u32[]{:S(2)}) copy-start(s32[4096]{0:T(1024)} %param.11) | copy-start | bytes 49156
Sparse Core Ops, SparseCore 0:
  10.1 66.9 all-gather.1
  81.4 67.6 reduce-scatter.1
where the time goes:
time: 259 us
  waiting for transfers between devices  137 us (53%)
  local copies, waits for them, and re-layouts  78.3 us (30%)
  starting transfers between devices  19.9 us (8%)
  between operations  18.5 us (7%)
  matrix products  4.17 us (2%)
    all_gather x1, waiting for transfers between devices, shards(): lax.all_gather(lambda_amps, 'col', axis=0, tiled=True)  68.1 us
    reduce_scatter x1, waiting for transfers between devices, shards(): lax.psum_scatter(partial_value, 'row', scatter_dimension=0, tiled=True)  67.7 us
    gather x1, local copies, waits for them, and re-layouts, shards(): jnp.take(virt_energy, col_orbitals[:, 0])  25.9 us
    gather x1, local copies, waits for them, and re-layouts, shards(): jnp.take(virt_energy, col_orbitals[:, 1])  25.9 us
    gather x1, local copies, waits for them, and re-layouts, shards(): anti = cycle - jnp.take(cycle, exchanged, axis=1)  23 us
    all_to_all x1, starting transfers between devices, shards(): lax.all_to_all(summed, 'col', split_axis=0, concat_axis=1, tiled=True)  19.8 us
  transfers between devices with their start and end apart: 3, of which 2 were waited for; matrix products, arithmetic and copies ran while one was open for 21% of the time, Pallas kernels for 0%

commit v1 on v0

v1 whole, which is shorter than its diff:
```python
import functools

import jax
import jax.numpy as jnp
from jax import lax
from jax.experimental import pallas as pl
from jax.experimental.pallas import tpu as pltpu
from jax.sharding import PartitionSpec as P

X, CORES, LANES = 4, 2, 128
VMEM = pltpu.VMEM
SMEM = pltpu.SMEM


def place(z, x, core):
    return (z * X + x % X) * CORES + core


def shift(dz=0, dx=0, dcore=0):
    return [
        (place(z, x, core), place(z ^ dz, x + dx, core ^ dcore))
        for z in range(2)
        for x in range(X)
        for core in range(CORES)
    ]


def lookup(table, where):
    row, lane = where // LANES, where % LANES
    found = jnp.zeros(where.shape, table.dtype)
    for k in range(table.shape[0]):
        line = jnp.broadcast_to(table[k : k + 1], where.shape)
        line = jnp.take_along_axis(line, lane, axis=1, mode="promise_in_bounds")
        found = jnp.where(row == k, line, found)
    return found


def denominators(virt_ref, col_ref, occ_ref, row_ref, out_ref):
    me = lax.axis_index("row") * lax.axis_size("col") + lax.axis_index("col")
    row_part = occ_ref[row_ref[0, me]] + occ_ref[row_ref[1, me]]
    for k in range(0, out_ref.shape[0], 8):
        first = lookup(virt_ref[...], col_ref[0, k : k + 8])
        second = lookup(virt_ref[...], col_ref[1, k : k + 8])
        out_ref[k : k + 8] = row_part - (first + second)


def halves(value):
    high = value.astype(jnp.bfloat16)
    return high, (value - high.astype(jnp.float32)).astype(jnp.bfloat16)


def product(block_refs, b_ref, a_ref):
    rows = block_refs[0].shape[0]
    total = rows * len(block_refs)
    for k, block in enumerate(block_refs):
        high, low = halves(block[...])
        a_ref[k * rows : (k + 1) * rows] = high
        a_ref[total + k * rows : total + (k + 1) * rows] = low
    b_high, b_low = halves(b_ref[...])
    both = jnp.dot(a_ref[...], b_high, preferred_element_type=jnp.float32)
    rest = jnp.dot(a_ref[:total], b_low, preferred_element_type=jnp.float32)
    return both[:total] + (both[total:] + rest)


def near(*refs):
    *blocks, b_ref, out_ref, a_ref = refs
    out_ref[...] = product(blocks, b_ref, a_ref)


def far(*refs):
    *blocks, b_ref, near_ref, out_ref, a_ref, done_ref = refs
    rows = blocks[0].shape[0]
    done_ref[...] = product(blocks, b_ref, a_ref)
    me = lax.axis_index("col")
    z, x, core = me // (X * CORES), (me // CORES) % X, me % CORES
    for ref, dz in ((near_ref, 0), (done_ref, 1)):
        for k in range(len(blocks)):
            source = place(z ^ dz, x + X - k % X, core ^ (k // X))
            for h in range(2):
                out_ref[pl.ds(source * (2 * rows) + h, rows, stride=2), :] = ref[
                    k * rows : (k + 1) * rows, h * LANES : (h + 1) * LANES
                ]


def finish(parts_ref, exchanged_ref, denom_ref, out_ref, cycle_ref):
    lines = out_ref.shape[0]
    total = parts_ref[:lines]
    for k in range(1, parts_ref.shape[0] // lines):
        total = total + parts_ref[k * lines : (k + 1) * lines]
    cycle_ref[...] = total
    for k in range(0, lines, 8):
        other = lookup(cycle_ref[...], exchanged_ref[k : k + 8])
        out_ref[k : k + 8] = (cycle_ref[k : k + 8] - other) / denom_ref[k : k + 8]


def shards(
    lambda_amps, cycle_inter, exchanged, occ_energy, virt_energy, row_orbitals, col_orbitals
):
    rows, depth = lambda_amps.shape
    window = exchanged.shape[0]
    width = cycle_inter.shape[1]
    lines = window // LANES
    f32 = functools.partial(jax.ShapeDtypeStruct, dtype=jnp.float32)
    v, s = pl.BlockSpec(memory_space=VMEM), pl.BlockSpec(memory_space=SMEM)

    def spread(block):
        line = [block] + [lax.ppermute(block, "col", shift(dx=k)) for k in (1, 2, 3)]
        return line + [lax.ppermute(part, "col", shift(dcore=1)) for part in line]

    swapped = lax.ppermute(lambda_amps, "col", shift(dz=1))
    near_blocks = spread(lambda_amps)
    denom = pl.pallas_call(
        denominators,
        out_shape=f32((lines, LANES)),
        in_specs=[v, v, s, s],
        out_specs=v,
    )(
        virt_energy.reshape(-1, LANES),
        col_orbitals.T.reshape(2, lines, LANES),
        occ_energy,
        row_orbitals.T,
    )
    count = len(near_blocks)
    split = pltpu.VMEM((2 * count * rows, depth), jnp.bfloat16)
    near_part = pl.pallas_call(
        near,
        out_shape=f32((count * rows, width)),
        in_specs=[v] * (count + 1),
        out_specs=v,
        scratch_shapes=[split],
    )(*near_blocks, cycle_inter)
    far_blocks = spread(swapped)
    parts = pl.pallas_call(
        far,
        out_shape=f32((4 * count * rows, LANES)),
        in_specs=[v] * (count + 2),
        out_specs=v,
        scratch_shapes=[split, pltpu.VMEM((count * rows, width), jnp.float32)],
    )(*far_blocks, cycle_inter, near_part)
    owners = lax.axis_size("row") * lax.axis_size("col")
    parts = lax.all_to_all(
        parts.reshape(owners, -1, LANES), ("row", "col"), 0, 0, tiled=True
    )
    update = pl.pallas_call(
        finish,
        out_shape=f32((lines, LANES)),
        in_specs=[v, v, v],
        out_specs=v,
        scratch_shapes=[pltpu.VMEM((lines, LANES), jnp.float32)],
    )(parts.reshape(-1, LANES), exchanged.reshape(lines, LANES), denom)
    return update.reshape(1, window)


def solution(mesh):
    placed = (P("col", "row"), P("row", "col"), P(), P(), P(), P(), P())
    return jax.shard_map(
        shards, mesh=mesh, in_specs=placed, out_specs=P(("row", "col"), None), check_vma=False
    )
```

time: 259 us -> 66.3 us (0.26)
  waiting for transfers between devices: 137 us -> 13.8 us
  local copies, waits for them, and re-layouts: 78.3 us -> 3.26 us
  starting transfers between devices: 19.9 us -> 38.8 us
  between operations: 18.5 us -> 0.16 us
  Pallas kernels: 0 us -> 10 us
  matrix products: 4.17 us -> 0 us
    gather x4 -> x0, local copies, waits for them, and re-layouts: 75.4 us -> none  [the longest x1 25.9 us: shards(): jnp.take(virt_energy, col_orbitals[:, 0])]
    all_gather x1 -> x0, waiting for transfers between devices: 68.1 us -> none  [shards(): lax.all_gather(lambda_amps, 'col', axis=0, tiled=True)]
    reduce_scatter x1 -> x0, waiting for transfers between devices: 67.7 us -> none  [shards(): lax.psum_scatter(partial_value, 'row', scatter_dimension=0, tiled=True)]
    ppermute x0 -> x15, starting transfers between devices: none -> 25.7 us  [the longest x8 10.7 us: spread(): return line + [lax.ppermute(part, 'col', shift(dcore=1)) for part in line]]
    all_to_all x1, waiting for transfers between devices: 0.01 us -> 13.3 us  [shards(): lax.all_to_all(parts.reshape(owners, -1, LANES), ('row', 'col'), 0, 0, ti...]
    pallas_call x0 -> x4, Pallas kernels: none -> 10 us  [the longest x1 3.32 us: shards(): pl.pallas_call(far, out_shape=f32((4 * count * rows, LANES)), in_specs=[v...]
    all_to_all x1, starting transfers between devices: 19.8 us -> 13.1 us  [shards(): lax.all_to_all(parts.reshape(owners, -1, LANES), ('row', 'col'), 0, 0, ti...]
    dot_general x1 -> x0, matrix products: 4.17 us -> none  [shards(): jnp.dot(lax.all_gather(lambda_amps, 'col', axis=0, tiled=True), cycle_int...]
  transfers between devices with their start and end apart: 3 -> 16, of which waited for: 2 -> 2; matrix products, arithmetic and copies ran while one was open for 21% -> 1% of each run, Pallas kernels for 0% -> 7%
where the time goes in v1:
time: 66.3 us; the launch traced here: 66.1 us
  starting transfers between devices  38.8 us (59%)
  waiting for transfers between devices  13.8 us (21%)
  Pallas kernels  10 us (15%)
  local copies, waits for them, and re-layouts  3.26 us (5%)
    all_to_all x1, waiting for transfers between devices, shards(): lax.all_to_all(parts.reshape(owners, -1, LANES), ('row', 'col'), 0, 0, ti...  13.3 us
    all_to_all x1, starting transfers between devices, shards(): lax.all_to_all(parts.reshape(owners, -1, LANES), ('row', 'col'), 0, 0, ti...  13.1 us
    ppermute x8, starting transfers between devices, spread(): return line + [lax.ppermute(part, 'col', shift(dcore=1)) for part in line]  10.7 us
    ppermute x6, starting transfers between devices, spread(): lax.ppermute(block, 'col', shift(dx=k))  8.12 us
    ppermute x1, starting transfers between devices, shards(): swapped = lax.ppermute(lambda_amps, 'col', shift(dz=1))  6.91 us
    pallas_call x1, Pallas kernels, shards(): pl.pallas_call(far, out_shape=f32((4 * count * rows, LANES)), in_specs=[v...  3.32 us
    pallas_call x1, Pallas kernels, shards(): pl.pallas_call(near, out_shape=f32((count * rows, width)), in_specs=[v] *...  3.28 us
    unnamed x35, local copies, waits for them, and re-layouts  3.26 us
  transfers between devices with their start and end apart: 16, of which 2 were waited for; matrix products, arithmetic and copies ran while one was open for 1% of the time, Pallas kernels for 7%

profile of v1, /device:TPU:1, one launch (start us, length us, event | category | flops | bytes accessed | tf_op | source)
XLA Modules:
  0.0 66.1 jit_solution(16409216383367165376)
XLA Ops:
  0.0 2.0 %collective-permute-start.8 = (f32[16,2048]{1,0:T(8,128)}, f32[16,2048]{1,0:T(8,128)S(1)}, u32[]{:S(2)}, u32[]{:S(2)}) collective-permute-start(f32[16,2048]{1,0:T(8,128)} %refs_0_.1), channel_id=1, source_target_pairs={{0,2},{1,3},{2,4},{3,5},{4,6},{5,7},{6,0},{7,1},{8,10},{9,11},{10,... | collective-permute-start | bytes 393224 | tf_op jit(solution)/shard_map/ppermute | solution.py:107
  2.0 2.5 %collective-permute-start.9 = (f32[16,2048]{1,0:T(8,128)}, f32[16,2048]{1,0:T(8,128)S(1)}, u32[]{:S(2)}, u32[]{:S(2)}) collective-permute-start(f32[16,2048]{1,0:T(8,128)} %refs_0_.1), channel_id=1, source_target_pairs={{0,4},{1,5},{2,6},{3,7},{4,0},{5,1},{6,2},{7,3},{8,12},{9,13},{10,... | collective-permute-start | bytes 393224 | tf_op jit(solution)/shard_map/ppermute | solution.py:107
  4.5 6.9 %collective-permute-start = (f32[16,2048]{1,0:T(8,128)}, f32[16,2048]{1,0:T(8,128)S(1)}, u32[]{:S(2)}, u32[]{:S(2)}) collective-permute-start(f32[16,2048]{1,0:T(8,128)} %refs_0_.1), channel_id=1, source_target_pairs={{0,8},{1,9},{2,10},{3,11},{4,12},{5,13},{6,14},{7,15},{8,0},{9,1},... | collective-permute-start | bytes 393224 | tf_op jit(solution)/shard_map/ppermute | solution.py:110
  11.4 1.2 %collective-permute-start.10 = (f32[16,2048]{1,0:T(8,128)}, f32[16,2048]{1,0:T(8,128)S(1)}, u32[]{:S(2)}, u32[]{:S(2)}) collective-permute-start(f32[16,2048]{1,0:T(8,128)} %refs_0_.1), channel_id=1, source_target_pairs={{0,6},{1,7},{2,0},{3,1},{4,2},{5,3},{6,4},{7,5},{8,14},{9,15},{10,... | collective-permute-start | bytes 393224 | tf_op jit(solution)/shard_map/ppermute | solution.py:107
  12.5 1.8 %collective-permute-start.11 = (f32[16,2048]{1,0:T(8,128)}, f32[16,2048]{1,0:T(8,128)S(1)}, u32[]{:S(2)}, u32[]{:S(2)}) collective-permute-start(f32[16,2048]{1,0:T(8,128)} %refs_0_.1), channel_id=1, source_target_pairs={{0,1},{1,0},{2,3},{3,2},{4,5},{5,4},{6,7},{7,6},{8,9},{9,8},{10,11... | collective-permute-start | bytes 393224 | tf_op jit(solution)/shard_map/ppermute | solution.py:108
  14.3 0.0 collective-permute-done.8.refs_1_
  14.3 0.0 copy-start.9
  14.3 0.1 collective-permute-start.12
  14.4 0.0 collective-permute-done.9.refs_2_
  14.4 0.0 copy-start.10
  14.4 0.4 collective-permute-start.13
  14.9 0.0 collective-permute-done.refs_0_
  14.9 0.0 copy-start.1
  14.9 0.3 collective-permute-start.1
  15.2 0.5 collective-permute-done.10.refs_3_
  15.7 0.7 %collective-permute-start.2 = (f32[16,2048]{1,0:T(8,128)S(1)}, f32[16,2048]{1,0:T(8,128)S(1)}, u32[]{:S(2)}, u32[]{:S(2)}) collective-permute-start(f32[16,2048]{1,0:T(8,128)S(1)} %collective-permute-done.refs_0_), channel_id=1, source_target_pairs={{0,4},{1,5},{2,6},{3,7},{4,0},{5,1},{6,2},{7,3},{8,12},{9,13},{10,... | collective-permute-start | bytes 393224 | tf_op jit(solution)/shard_map/ppermute | solution.py:107
  16.4 0.0 collective-permute-done.11.refs_4_
  16.4 0.0 copy-start.12
  16.4 1.4 %collective-permute-start.3 = (f32[16,2048]{1,0:T(8,128)S(1)}, f32[16,2048]{1,0:T(8,128)S(1)}, u32[]{:S(2)}, u32[]{:S(2)}) collective-permute-start(f32[16,2048]{1,0:T(8,128)S(1)} %collective-permute-done.refs_0_), channel_id=1, source_target_pairs={{0,6},{1,7},{2,0},{3,1},{4,2},{5,3},{6,4},{7,5},{8,14},{9,15},{10,... | collective-permute-start | bytes 393224 | tf_op jit(solution)/shard_map/ppermute | solution.py:107
  17.9 0.0 collective-permute-done.12.refs_5_
  17.9 0.0 copy-start.13
  17.9 3.4 %collective-permute-start.4 = (f32[16,2048]{1,0:T(8,128)S(1)}, f32[16,2048]{1,0:T(8,128)S(1)}, u32[]{:S(2)}, u32[]{:S(2)}) collective-permute-start(f32[16,2048]{1,0:T(8,128)S(1)} %collective-permute-done.refs_0_), channel_id=1, source_target_pairs={{0,1},{1,0},{2,3},{3,2},{4,5},{5,4},{6,7},{7,6},{8,9},{9,8},{10,11... | collective-permute-start | bytes 393224 | tf_op jit(solution)/shard_map/ppermute | solution.py:108
  21.2 0.0 collective-permute-done.13.refs_6_
  21.2 0.0 copy-start.14
  21.2 0.1 collective-permute-start.14
  21.4 0.0 collective-permute-done.1.refs_1_
  21.4 0.0 copy-start.2
  21.4 4.0 %collective-permute-start.5 = (f32[16,2048]{1,0:T(8,128)S(1)}, f32[16,2048]{1,0:T(8,128)S(1)}, u32[]{:S(2)}, u32[]{:S(2)}) collective-permute-start(f32[16,2048]{1,0:T(8,128)S(1)} %collective-permute-done.1.refs_1_), channel_id=1, source_target_pairs={{0,1},{1,0},{2,3},{3,2},{4,5},{5,4},{6,7},{7,6},{8,9},{9,8},{10,11... | collective-permute-start | bytes 393224 | tf_op jit(solution)/shard_map/ppermute | solution.py:108
  25.4 0.0 collective-permute-done.2.refs_2_
  25.4 0.1 collective-permute-start.6
  25.5 0.0 collective-permute-done.3.refs_3_
  25.5 0.8 %collective-permute-start.7 = (f32[16,2048]{1,0:T(8,128)S(1)}, f32[16,2048]{1,0:T(8,128)S(1)}, u32[]{:S(2)}, u32[]{:S(2)}) collective-permute-start(f32[16,2048]{1,0:T(8,128)S(1)} %collective-permute-done.3.refs_3_), channel_id=1, source_target_pairs={{0,1},{1,0},{2,3},{3,2},{4,5},{5,4},{6,7},{7,6},{8,9},{9,8},{10,11... | collective-permute-start | bytes 393224 | tf_op jit(solution)/shard_map/ppermute | solution.py:108
  26.3 0.0 collective-permute-done.14.refs_7_
  26.3 0.0 copy-done.9
  26.3 0.0 copy-done.10
  26.3 0.0 copy-done.11
  26.3 0.0 copy-done.12
  26.3 0.0 copy-done.13
  26.3 0.0 copy-done.14
  26.3 0.0 copy-start.15
  26.3 0.6 copy-done.15
  27.0 3.3 %shard_map.73.refs_9_ = f32[128,256]{1,0:T(8,128)} custom-call(f32[16,2048]{1,0:T(8,128)} %refs_0_.1, f32[16,2048]{1,0:T(8,128)} %copy-done.9, f32[16,2048]{1,0:T(8,128)} %copy-done.10, f32[16,2048]{1,0:T(8,128)} %copy-done.11, f32[16,2048]{1,0:T(8,128)} %copy-done.12, f32[16,2048]{1,0:T(8,128)} %copy-done.13, f32[16,2048]{1,0:T(8,128)} %copy-done.14, ...), custom_call_target="tpu_custom_call" | custom-call | tf_op jit(solution)/shard_map/pallas_call | solution.py:125
  30.3 0.0 collective-permute-done.4.refs_4_
  30.3 0.0 collective-permute-done.5.refs_5_
  30.3 0.0 copy-start.6
  30.3 0.0 collective-permute-done.6.refs_6_
  30.3 0.0 copy-start.7
  30.3 0.0 collective-permute-done.7.refs_7_
  30.3 0.0 copy-done.1
  30.3 0.0 copy-done.2
  30.3 0.0 copy-done.3
  30.3 0.0 copy-done.4
  30.4 0.6 copy-done.5
  30.9 0.0 copy-done.6
  31.0 0.1 copy-done.7
  31.0 0.6 copy-done.8
  31.7 3.3 %shard_map.74 = f32[512,128]{1,0:T(8,128)} custom-call(f32[16,2048]{1,0:T(8,128)} %copy-done.1, f32[16,2048]{1,0:T(8,128)} %copy-done.2, f32[16,2048]{1,0:T(8,128)} %copy-done.3, f32[16,2048]{1,0:T(8,128)} %copy-done.4, f32[16,2048]{1,0:T(8,128)} %copy-done.5, f32[16,2048]{1,0:T(8,128)} %copy-done.6, f32[16,2048]{1,0:T(8,128)} %copy-done.7, ...), custom_call_target="tpu_custom_call" | custom-call | tf_op jit(solution)/shard_map/pallas_call | solution.py:133
  35.0 13.1 %all-to-all-start = ((f32[256,2,128]{2,1,0:T(2,128)}), f32[256,2,128]{2,1,0:T(2,128)S(1)}, u32[]{:S(2)}, u32[]{:S(2)}) async-start(f32[256,2,128]{2,1,0:T(2,128)} %bitcast.11), calls=%async_computation | async-start | bytes 524288 | tf_op jit(solution)/shard_map/all_to_all | solution.py:141
  48.1 0.0 copy-done.16
  48.1 0.6 copy.10
  48.7 1.6 %shard_map.75.denom_ref = f32[32,128]{1,0:T(8,128)} custom-call(f32[4,128]{1,0:T(4,128)} %bitcast.16, s32[2,32,128]{2,1,0:T(8,128)} %bitcast.13, f32[64]{0:T(128)} %occ_ref.1, s32[2,256]{1,0:T(2,128)} %bitcast.17), custom_call_target="tpu_custom_call" | custom-call | tf_op jit(solution)/shard_map/pallas_call | solution.py:112
  50.3 13.3 %all-to-all-done = f32[256,2,128]{2,1,0:T(2,128)S(1)} async-done(((f32[256,2,128]{2,1,0:T(2,128)}), f32[256,2,128]{2,1,0:T(2,128)S(1)}, u32[]{:S(2)}, u32[]{:S(2)}) %all-to-all-start) | async-done | bytes 262176 | tf_op jit(solution)/shard_map/all_to_all | solution.py:141
  63.6 0.7 %copy-done = f32[256,2,128]{2,1,0:T(2,128)} copy-done((f32[256,2,128]{2,1,0:T(2,128)}, f32[256,2,128]{2,1,0:T(2,128)S(1)}, u32[]{:S(2)}) %copy-start) | copy-done | bytes 262168
  64.2 1.8 %shard_map.76 = f32[32,128]{1,0:T(8,128)} custom-call(f32[512,128]{1,0:T(8,128)} %bitcast.12, s32[32,128]{1,0:T(8,128)} %bitcast.15, f32[32,128]{1,0:T(8,128)} %shard_map.75.denom_ref), custom_call_target="tpu_custom_call" | custom-call | tf_op jit(solution)/shard_map/pallas_call | solution.py:144
  (7 shorter events, 0.0 us)
Async XLA Ops:
  0.0 14.3 %collective-permute-start.8 = (f32[16,2048]{1,0:T(8,128)}, f32[16,2048]{1,0:T(8,128)S(1)}, u32[]{:S(2)}, u32[]{:S(2)}) collective-permute-start(f32[16,2048]{1,0:T(8,128)} %refs_0_.1), channel_id=1, source_target_pairs={{0,2},{1,3},{2,4},{3,5},{4,6},{5,7},{6,0},{7,1},{8,10},{9,11},{10,... | collective-permute-start | bytes 393224 | tf_op jit(solution)/shard_map/ppermute | solution.py:107
  2.0 12.4 %collective-permute-start.9 = (f32[16,2048]{1,0:T(8,128)}, f32[16,2048]{1,0:T(8,128)S(1)}, u32[]{:S(2)}, u32[]{:S(2)}) collective-permute-start(f32[16,2048]{1,0:T(8,128)} %refs_0_.1), channel_id=1, source_target_pairs={{0,4},{1,5},{2,6},{3,7},{4,0},{5,1},{6,2},{7,3},{8,12},{9,13},{10,... | collective-permute-start | bytes 393224 | tf_op jit(solution)/shard_map/ppermute | solution.py:107
  4.5 10.4 %collective-permute-start = (f32[16,2048]{1,0:T(8,128)}, f32[16,2048]{1,0:T(8,128)S(1)}, u32[]{:S(2)}, u32[]{:S(2)}) collective-permute-start(f32[16,2048]{1,0:T(8,128)} %refs_0_.1), channel_id=1, source_target_pairs={{0,8},{1,9},{2,10},{3,11},{4,12},{5,13},{6,14},{7,15},{8,0},{9,1},... | collective-permute-start | bytes 393224 | tf_op jit(solution)/shard_map/ppermute | solution.py:110
  11.4 4.3 %collective-permute-start.10 = (f32[16,2048]{1,0:T(8,128)}, f32[16,2048]{1,0:T(8,128)S(1)}, u32[]{:S(2)}, u32[]{:S(2)}) collective-permute-start(f32[16,2048]{1,0:T(8,128)} %refs_0_.1), channel_id=1, source_target_pairs={{0,6},{1,7},{2,0},{3,1},{4,2},{5,3},{6,4},{7,5},{8,14},{9,15},{10,... | collective-permute-start | bytes 393224 | tf_op jit(solution)/shard_map/ppermute | solution.py:107
  12.5 3.9 %collective-permute-start.11 = (f32[16,2048]{1,0:T(8,128)}, f32[16,2048]{1,0:T(8,128)S(1)}, u32[]{:S(2)}, u32[]{:S(2)}) collective-permute-start(f32[16,2048]{1,0:T(8,128)} %refs_0_.1), channel_id=1, source_target_pairs={{0,1},{1,0},{2,3},{3,2},{4,5},{5,4},{6,7},{7,6},{8,9},{9,8},{10,11... | collective-permute-start | bytes 393224 | tf_op jit(solution)/shard_map/ppermute | solution.py:108
  14.3 11.9 %copy-start.9 = (f32[16,2048]{1,0:T(8,128)}, f32[16,2048]{1,0:T(8,128)S(1)}, u32[]{:S(2)}) copy-start(f32[16,2048]{1,0:T(8,128)S(1)} %collective-permute-done.8.refs_1_) | copy-start | bytes 393220
  14.3 3.5 %collective-permute-start.12 = (f32[16,2048]{1,0:T(8,128)S(1)}, f32[16,2048]{1,0:T(8,128)S(1)}, u32[]{:S(2)}, u32[]{:S(2)}) collective-permute-start(f32[16,2048]{1,0:T(8,128)S(1)} %collective-permute-done.8.refs_1_), channel_id=1, source_target_pairs={{0,1},{1,0},{2,3},{3,2},{4,5},{5,4},{6,7},{7,6},{8,9},{9,8},{10,11... | collective-permute-start | bytes 393224 | tf_op jit(solution)/shard_map/ppermute | solution.py:108
  14.4 11.8 %copy-start.10 = (f32[16,2048]{1,0:T(8,128)}, f32[16,2048]{1,0:T(8,128)S(1)}, u32[]{:S(2)}) copy-start(f32[16,2048]{1,0:T(8,128)S(1)} %collective-permute-done.9.refs_2_) | copy-start | bytes 393220
  14.4 6.8 %collective-permute-start.13 = (f32[16,2048]{1,0:T(8,128)S(1)}, f32[16,2048]{1,0:T(8,128)S(1)}, u32[]{:S(2)}, u32[]{:S(2)}) collective-permute-start(f32[16,2048]{1,0:T(8,128)S(1)} %collective-permute-done.9.refs_2_), channel_id=1, source_target_pairs={{0,1},{1,0},{2,3},{3,2},{4,5},{5,4},{6,7},{7,6},{8,9},{9,8},{10,11... | collective-permute-start | bytes 393224 | tf_op jit(solution)/shard_map/ppermute | solution.py:108
  14.9 15.5 %copy-start.1 = (f32[16,2048]{1,0:T(8,128)}, f32[16,2048]{1,0:T(8,128)S(1)}, u32[]{:S(2)}) copy-start(f32[16,2048]{1,0:T(8,128)S(1)} %collective-permute-done.refs_0_) | copy-start | bytes 393220
  14.9 6.5 %collective-permute-start.1 = (f32[16,2048]{1,0:T(8,128)S(1)}, f32[16,2048]{1,0:T(8,128)S(1)}, u32[]{:S(2)}, u32[]{:S(2)}) collective-permute-start(f32[16,2048]{1,0:T(8,128)S(1)} %collective-permute-done.refs_0_), channel_id=1, source_target_pairs={{0,2},{1,3},{2,4},{3,5},{4,6},{5,7},{6,0},{7,1},{8,10},{9,11},{10,... | collective-permute-start | bytes 393224 | tf_op jit(solution)/shard_map/ppermute | solution.py:107
  15.7 10.6 %copy-start.11 = (f32[16,2048]{1,0:T(8,128)}, f32[16,2048]{1,0:T(8,128)S(1)}, u32[]{:S(2)}) copy-start(f32[16,2048]{1,0:T(8,128)S(1)} %collective-permute-done.10.refs_3_) | copy-start | bytes 393220
  15.7 9.7 %collective-permute-start.2 = (f32[16,2048]{1,0:T(8,128)S(1)}, f32[16,2048]{1,0:T(8,128)S(1)}, u32[]{:S(2)}, u32[]{:S(2)}) collective-permute-start(f32[16,2048]{1,0:T(8,128)S(1)} %collective-permute-done.refs_0_), channel_id=1, source_target_pairs={{0,4},{1,5},{2,6},{3,7},{4,0},{5,1},{6,2},{7,3},{8,12},{9,13},{10,... | collective-permute-start | bytes 393224 | tf_op jit(solution)/shard_map/ppermute | solution.py:107
  16.4 9.9 %copy-start.12 = (f32[16,2048]{1,0:T(8,128)}, f32[16,2048]{1,0:T(8,128)S(1)}, u32[]{:S(2)}) copy-start(f32[16,2048]{1,0:T(8,128)S(1)} %collective-permute-done.11.refs_4_) | copy-start | bytes 393220
  16.4 9.0 %collective-permute-start.3 = (f32[16,2048]{1,0:T(8,128)S(1)}, f32[16,2048]{1,0:T(8,128)S(1)}, u32[]{:S(2)}, u32[]{:S(2)}) collective-permute-start(f32[16,2048]{1,0:T(8,128)S(1)} %collective-permute-done.refs_0_), channel_id=1, source_target_pairs={{0,6},{1,7},{2,0},{3,1},{4,2},{5,3},{6,4},{7,5},{8,14},{9,15},{10,... | collective-permute-start | bytes 393224 | tf_op jit(solution)/shard_map/ppermute | solution.py:107
  17.9 8.4 %copy-start.13 = (f32[16,2048]{1,0:T(8,128)}, f32[16,2048]{1,0:T(8,128)S(1)}, u32[]{:S(2)}) copy-start(f32[16,2048]{1,0:T(8,128)S(1)} %collective-permute-done.12.refs_5_) | copy-start | bytes 393220
  17.9 12.4 %collective-permute-start.4 = (f32[16,2048]{1,0:T(8,128)S(1)}, f32[16,2048]{1,0:T(8,128)S(1)}, u32[]{:S(2)}, u32[]{:S(2)}) collective-permute-start(f32[16,2048]{1,0:T(8,128)S(1)} %collective-permute-done.refs_0_), channel_id=1, source_target_pairs={{0,1},{1,0},{2,3},{3,2},{4,5},{5,4},{6,7},{7,6},{8,9},{9,8},{10,11... | collective-permute-start | bytes 393224 | tf_op jit(solution)/shard_map/ppermute | solution.py:108
  21.2 5.1 %copy-start.14 = (f32[16,2048]{1,0:T(8,128)}, f32[16,2048]{1,0:T(8,128)S(1)}, u32[]{:S(2)}) copy-start(f32[16,2048]{1,0:T(8,128)S(1)} %collective-permute-done.13.refs_6_) | copy-start | bytes 393220
  21.2 5.0 %collective-permute-start.14 = (f32[16,2048]{1,0:T(8,128)S(1)}, f32[16,2048]{1,0:T(8,128)S(1)}, u32[]{:S(2)}, u32[]{:S(2)}) collective-permute-start(f32[16,2048]{1,0:T(8,128)S(1)} %collective-permute-done.10.refs_3_), channel_id=1, source_target_pairs={{0,1},{1,0},{2,3},{3,2},{4,5},{5,4},{6,7},{7,6},{8,9},{9,8},{10,11... | collective-permute-start | bytes 393224 | tf_op jit(solution)/shard_map/ppermute | solution.py:108
  21.4 9.0 %copy-start.2 = (f32[16,2048]{1,0:T(8,128)}, f32[16,2048]{1,0:T(8,128)S(1)}, u32[]{:S(2)}) copy-start(f32[16,2048]{1,0:T(8,128)S(1)} %collective-permute-done.1.refs_1_) | copy-start | bytes 393220
  21.4 8.9 %collective-permute-start.5 = (f32[16,2048]{1,0:T(8,128)S(1)}, f32[16,2048]{1,0:T(8,128)S(1)}, u32[]{:S(2)}, u32[]{:S(2)}) collective-permute-start(f32[16,2048]{1,0:T(8,128)S(1)} %collective-permute-done.1.refs_1_), channel_id=1, source_target_pairs={{0,1},{1,0},{2,3},{3,2},{4,5},{5,4},{6,7},{7,6},{8,9},{9,8},{10,11... | collective-permute-start | bytes 393224 | tf_op jit(solution)/shard_map/ppermute | solution.py:108
  25.4 5.0 %copy-start.3 = (f32[16,2048]{1,0:T(8,128)}, f32[16,2048]{1,0:T(8,128)S(1)}, u32[]{:S(2)}) copy-start(f32[16,2048]{1,0:T(8,128)S(1)} %collective-permute-done.2.refs_2_) | copy-start | bytes 393220
  25.4 4.9 %collective-permute-start.6 = (f32[16,2048]{1,0:T(8,128)S(1)}, f32[16,2048]{1,0:T(8,128)S(1)}, u32[]{:S(2)}, u32[]{:S(2)}) collective-permute-start(f32[16,2048]{1,0:T(8,128)S(1)} %collective-permute-done.2.refs_2_), channel_id=1, source_target_pairs={{0,1},{1,0},{2,3},{3,2},{4,5},{5,4},{6,7},{7,6},{8,9},{9,8},{10,11... | collective-permute-start | bytes 393224 | tf_op jit(solution)/shard_map/ppermute | solution.py:108
  25.5 4.9 %copy-start.4 = (f32[16,2048]{1,0:T(8,128)}, f32[16,2048]{1,0:T(8,128)S(1)}, u32[]{:S(2)}) copy-start(f32[16,2048]{1,0:T(8,128)S(1)} %collective-permute-done.3.refs_3_) | copy-start | bytes 393220
  25.5 4.8 %collective-permute-start.7 = (f32[16,2048]{1,0:T(8,128)S(1)}, f32[16,2048]{1,0:T(8,128)S(1)}, u32[]{:S(2)}, u32[]{:S(2)}) collective-permute-start(f32[16,2048]{1,0:T(8,128)S(1)} %collective-permute-done.3.refs_3_), channel_id=1, source_target_pairs={{0,1},{1,0},{2,3},{3,2},{4,5},{5,4},{6,7},{7,6},{8,9},{9,8},{10,11... | collective-permute-start | bytes 393224 | tf_op jit(solution)/shard_map/ppermute | solution.py:108
  26.3 0.6 copy-start.15
  30.3 17.8 %copy-start.16 = (s32[4096,2]{0,1:T(2,128)S(1)}, s32[4096,2]{0,1:T(2,128)}, u32[]{:S(2)}) copy-start(s32[4096,2]{0,1:T(2,128)} %param.13) | copy-start | bytes 98308
  30.3 0.6 copy-start.5
  30.3 0.7 %copy-start.6 = (f32[16,2048]{1,0:T(8,128)}, f32[16,2048]{1,0:T(8,128)S(1)}, u32[]{:S(2)}) copy-start(f32[16,2048]{1,0:T(8,128)S(1)} %collective-permute-done.5.refs_5_) | copy-start | bytes 393220
  30.3 0.7 %copy-start.7 = (f32[16,2048]{1,0:T(8,128)}, f32[16,2048]{1,0:T(8,128)S(1)}, u32[]{:S(2)}) copy-start(f32[16,2048]{1,0:T(8,128)S(1)} %collective-permute-done.6.refs_6_) | copy-start | bytes 393220
  31.0 0.6 copy-start.8
  35.0 28.6 %all-to-all-start = ((f32[256,2,128]{2,1,0:T(2,128)}), f32[256,2,128]{2,1,0:T(2,128)S(1)}, u32[]{:S(2)}, u32[]{:S(2)}) async-start(f32[256,2,128]{2,1,0:T(2,128)} %bitcast.11), calls=%async_computation | async-start | bytes 524288 | tf_op jit(solution)/shard_map/all_to_all | solution.py:141
  63.6 0.7 %copy-start = (f32[256,2,128]{2,1,0:T(2,128)}, f32[256,2,128]{2,1,0:T(2,128)S(1)}, u32[]{:S(2)}) copy-start(f32[256,2,128]{2,1,0:T(2,128)S(1)} %all-to-all-done) | copy-start | bytes 786436

commit v2 on v1

v2 whole, which is shorter than its diff:
```python
import jax
import jax.numpy as jnp
from jax import lax
from jax.experimental import pallas as pl
from jax.experimental.pallas import tpu as pltpu
from jax.sharding import PartitionSpec as P

X, CORES, LANES = 4, 2, 128
VMEM = pltpu.VMEM
SMEM = pltpu.SMEM
LIMIT = pltpu.CompilerParams(vmem_limit_bytes=24 << 20)


def place(z, x, core):
    return (z * X + x % X) * CORES + core


def shift(dz=0, dx=0, dcore=0):
    return [
        (place(z, x, core), place(z ^ dz, x + dx, core ^ dcore))
        for z in range(2)
        for x in range(X)
        for core in range(CORES)
    ]


def lookup(table, where):
    row, lane = where // LANES, where % LANES
    found = jnp.zeros(where.shape, table.dtype)
    for k in range(table.shape[0]):
        line = jnp.broadcast_to(table[k : k + 1], where.shape)
        line = jnp.take_along_axis(line, lane, axis=1, mode="promise_in_bounds")
        found = jnp.where(row == k, line, found)
    return found


def halves(value):
    high = value.astype(jnp.bfloat16)
    return high, (value - high.astype(jnp.float32)).astype(jnp.bfloat16)


def prepare(virt_ref, col_ref, occ_ref, row_ref, b_ref, denom_ref, high_ref, low_ref):
    high_ref[...], low_ref[...] = halves(b_ref[...])
    me = lax.axis_index("row") * lax.axis_size("col") + lax.axis_index("col")
    row_part = occ_ref[row_ref[0, me]] + occ_ref[row_ref[1, me]]
    for k in range(denom_ref.shape[0]):
        lanes = slice(k * LANES, (k + 1) * LANES)
        pair = lookup(virt_ref[...], col_ref[:, lanes])
        denom_ref[k : k + 1] = row_part - (pair[:1] + pair[1:])


def product(block_refs, high_ref, low_ref, a_ref):
    rows = block_refs[0].shape[0]
    total = rows * len(block_refs)
    for k, block in enumerate(block_refs):
        high, low = halves(block[...])
        a_ref[k * rows : (k + 1) * rows] = high
        a_ref[total + k * rows : total + (k + 1) * rows] = low
    both = jnp.dot(a_ref[...], high_ref[...], preferred_element_type=jnp.float32)
    rest = jnp.dot(a_ref[:total], low_ref[...], preferred_element_type=jnp.float32)
    return both[:total] + (both[total:] + rest)


def near(*refs):
    *blocks, high_ref, low_ref, out_ref, a_ref = refs
    out_ref[...] = product(blocks, high_ref, low_ref, a_ref)


def far(*refs):
    *blocks, high_ref, low_ref, near_ref, out_ref, a_ref, done_ref = refs
    rows = blocks[0].shape[0]
    done_ref[...] = product(blocks, high_ref, low_ref, a_ref)
    me = lax.axis_index("col")
    z, x, core = me // (X * CORES), (me // CORES) % X, me % CORES
    for ref, dz in ((near_ref, 0), (done_ref, 1)):
        for k in range(len(blocks)):
            source = place(z ^ dz, x + X - k % X, core ^ (k // X))
            for h in range(2):
                out_ref[pl.ds(source * (2 * rows) + h, rows, stride=2), :] = ref[
                    k * rows : (k + 1) * rows, h * LANES : (h + 1) * LANES
                ]


def finish(parts_ref, exchanged_ref, denom_ref, out_ref, cycle_ref):
    lines = out_ref.shape[0]
    total = parts_ref[:lines]
    for k in range(1, parts_ref.shape[0] // lines):
        total = total + parts_ref[k * lines : (k + 1) * lines]
    cycle_ref[...] = total
    for k in range(0, lines, 8):
        other = lookup(cycle_ref[...], exchanged_ref[k : k + 8])
        out_ref[k : k + 8] = (cycle_ref[k : k + 8] - other) / denom_ref[k : k + 8]


def shards(
    lambda_amps, cycle_inter, exchanged, occ_energy, virt_energy, row_orbitals, col_orbitals
):
    rows, depth = lambda_amps.shape
    window = exchanged.shape[0]
    width = cycle_inter.shape[1]
    lines = window // LANES
    count = X * CORES
    v, s = pl.BlockSpec(memory_space=VMEM), pl.BlockSpec(memory_space=SMEM)
    split = VMEM((2 * count * rows, depth), jnp.bfloat16)

    def here(value):
        return pltpu.with_memory_space_constraint(value, VMEM)

    def send(block, **by):
        return lax.ppermute(block, "col", shift(**by))

    def spread(block):
        line = [block] + [send(block, dx=k) for k in (1, 2, 3)]
        return line + [send(part, dcore=1) for part in line]

    swapped = send(lambda_amps, dz=1)
    near_blocks = spread(lambda_amps)
    denom, high, low = pl.pallas_call(
        prepare,
        out_shape=(
            VMEM((lines, LANES), jnp.float32),
            VMEM(cycle_inter.shape, jnp.bfloat16),
            VMEM(cycle_inter.shape, jnp.bfloat16),
        ),
        in_specs=[v, v, s, s, v],
        out_specs=(v, v, v),
        compiler_params=LIMIT,
    )(
        virt_energy.reshape(-1, LANES),
        col_orbitals.T,
        occ_energy,
        row_orbitals.T,
        here(cycle_inter),
    )
    near_part = pl.pallas_call(
        near,
        out_shape=VMEM((count * rows, width), jnp.float32),
        in_specs=[v] * (count + 2),
        out_specs=v,
        scratch_shapes=[split],
        compiler_params=LIMIT,
    )(*map(here, near_blocks), here(high), here(low))
    far_blocks = spread(swapped)
    parts = pl.pallas_call(
        far,
        out_shape=VMEM((4 * count * rows, LANES), jnp.float32),
        in_specs=[v] * (count + 3),
        out_specs=v,
        scratch_shapes=[split, VMEM((count * rows, width), jnp.float32)],
        compiler_params=LIMIT,
    )(*map(here, far_blocks), here(high), here(low), here(near_part))
    owners = lax.axis_size("row") * lax.axis_size("col")
    parts = lax.all_to_all(
        parts.reshape(owners, -1, LANES), ("row", "col"), 0, 0, tiled=True
    )
    update = pl.pallas_call(
        finish,
        out_shape=jax.ShapeDtypeStruct((lines, LANES), jnp.float32),
        in_specs=[v, v, v],
        out_specs=v,
        scratch_shapes=[VMEM((lines, LANES), jnp.float32)],
        compiler_params=LIMIT,
    )(here(parts.reshape(-1, LANES)), exchanged.reshape(lines, LANES), here(denom))
    return update.reshape(1, window)


def solution(mesh):
    placed = (P("col", "row"), P("row", "col"), P(), P(), P(), P(), P())

    return jax.shard_map(
        shards, mesh=mesh, in_specs=placed, out_specs=P(("row", "col"), None), check_vma=False
    )
```

time: 66.3 us -> 62.9 us (0.949)
  blocking collectives: 0 us -> 28.4 us
  waiting for transfers between devices: 13.8 us -> 0.56 us
  starting transfers between devices: 38.8 us -> 25.7 us
  Pallas kernels: 10 us -> 3.47 us
  local copies, waits for them, and re-layouts: 3.26 us -> 4.37 us
    all_to_all x0 -> x1, blocking collectives: none -> 28.4 us  [shards(): lax.all_to_all(parts.reshape(owners, -1, LANES), ('row', 'col'), 0, 0, ti...]
    all_to_all x1 -> x0, waiting for transfers between devices: 13.3 us -> none  [shards(): lax.all_to_all(parts.reshape(owners, -1, LANES), ('row', 'col'), 0, 0, ti...]
    all_to_all x1 -> x0, starting transfers between devices: 13.1 us -> none  [shards(): lax.all_to_all(parts.reshape(owners, -1, LANES), ('row', 'col'), 0, 0, ti...]
    pallas_call x4, Pallas kernels: 10 us -> 3.47 us  [the longest x1 1.44 us: shards(): pl.pallas_call(prepare, out_shape=(VMEM((lines, LANES), jnp.float32), VME...]
    unnamed x35 -> x14, local copies, waits for them, and re-layouts: 3.26 us -> 4.37 us
  transfers between devices with their start and end apart: 16 -> 15, of which waited for: 2 -> 1; matrix products, arithmetic and copies ran while one was open for 1% -> 0% of each run, Pallas kernels for 7% -> 3%
where the time goes in v2:
time: 62.9 us; the launch traced here: 62.6 us
  blocking collectives  28.4 us (45%)
  starting transfers between devices  25.7 us (41%)
  local copies, waits for them, and re-layouts  4.37 us (7%)
  Pallas kernels  3.47 us (6%)
    all_to_all x1, blocking collectives, shards(): lax.all_to_all(parts.reshape(owners, -1, LANES), ('row', 'col'), 0, 0, ti...  28.4 us
    ppermute x15, starting transfers between devices, send(): return lax.ppermute(block, 'col', shift(**by))  25.7 us
    unnamed x14, local copies, waits for them, and re-layouts  4.37 us
    pallas_call x1, Pallas kernels, shards(): pl.pallas_call(prepare, out_shape=(VMEM((lines, LANES), jnp.float32), VME...  1.44 us
  transfers between devices with their start and end apart: 15, of which 1 were waited for; matrix products, arithmetic and copies ran while one was open for 0% of the time, Pallas kernels for 3%

profile of v2, /device:TPU:1, one launch (start us, length us, event | category | flops | bytes accessed | tf_op | source)
XLA Modules:
  0.0 62.6 jit_solution(7021621058638457621)
XLA Ops:
  0.0 2.0 %collective-permute-start.8 = (f32[16,2048]{1,0:T(8,128)}, f32[16,2048]{1,0:T(8,128)S(1)}, u32[]{:S(2)}, u32[]{:S(2)}) collective-permute-start(f32[16,2048]{1,0:T(8,128)} %refs_0_.1), channel_id=1, source_target_pairs={{0,2},{1,3},{2,4},{3,5},{4,6},{5,7},{6,0},{7,1},{8,10},{9,11},{10,... | collective-permute-start | bytes 393224 | tf_op jit(solution)/shard_map/ppermute | solution.py:110
  2.0 2.5 %collective-permute-start.9 = (f32[16,2048]{1,0:T(8,128)}, f32[16,2048]{1,0:T(8,128)S(1)}, u32[]{:S(2)}, u32[]{:S(2)}) collective-permute-start(f32[16,2048]{1,0:T(8,128)} %refs_0_.1), channel_id=1, source_target_pairs={{0,4},{1,5},{2,6},{3,7},{4,0},{5,1},{6,2},{7,3},{8,12},{9,13},{10,... | collective-permute-start | bytes 393224 | tf_op jit(solution)/shard_map/ppermute | solution.py:110
  4.5 6.9 %collective-permute-start = (f32[16,2048]{1,0:T(8,128)}, f32[16,2048]{1,0:T(8,128)S(1)}, u32[]{:S(2)}, u32[]{:S(2)}) collective-permute-start(f32[16,2048]{1,0:T(8,128)} %refs_0_.1), channel_id=1, source_target_pairs={{0,8},{1,9},{2,10},{3,11},{4,12},{5,13},{6,14},{7,15},{8,0},{9,1},... | collective-permute-start | bytes 393224 | tf_op jit(solution)/shard_map/ppermute | solution.py:110
  11.4 1.2 %collective-permute-start.10 = (f32[16,2048]{1,0:T(8,128)}, f32[16,2048]{1,0:T(8,128)S(1)}, u32[]{:S(2)}, u32[]{:S(2)}) collective-permute-start(f32[16,2048]{1,0:T(8,128)} %refs_0_.1), channel_id=1, source_target_pairs={{0,6},{1,7},{2,0},{3,1},{4,2},{5,3},{6,4},{7,5},{8,14},{9,15},{10,... | collective-permute-start | bytes 393224 | tf_op jit(solution)/shard_map/ppermute | solution.py:110
  12.5 1.8 %collective-permute-start.11 = (f32[16,2048]{1,0:T(8,128)}, f32[16,2048]{1,0:T(8,128)S(1)}, u32[]{:S(2)}, u32[]{:S(2)}) collective-permute-start(f32[16,2048]{1,0:T(8,128)} %refs_0_.1), channel_id=1, source_target_pairs={{0,1},{1,0},{2,3},{3,2},{4,5},{5,4},{6,7},{7,6},{8,9},{9,8},{10,11... | collective-permute-start | bytes 393224 | tf_op jit(solution)/shard_map/ppermute | solution.py:110
  14.3 0.0 collective-permute-done.8.refs_1_
  14.3 0.0 collective-permute-start.12
  14.3 0.0 collective-permute-done.9.refs_2_
  14.4 0.5 collective-permute-start.13
  14.9 0.0 collective-permute-done.refs_0_
  14.9 0.3 collective-permute-start.1
  15.2 0.5 collective-permute-done.10.refs_3_
  15.7 0.7 %collective-permute-start.2 = (f32[16,2048]{1,0:T(8,128)S(1)}, f32[16,2048]{1,0:T(8,128)S(1)}, u32[]{:S(2)}, u32[]{:S(2)}) collective-permute-start(f32[16,2048]{1,0:T(8,128)S(1)} %collective-permute-done.refs_0_), channel_id=1, source_target_pairs={{0,4},{1,5},{2,6},{3,7},{4,0},{5,1},{6,2},{7,3},{8,12},{9,13},{10,... | collective-permute-start | bytes 393224 | tf_op jit(solution)/shard_map/ppermute | solution.py:110
  16.4 0.0 collective-permute-done.11.refs_4_
  16.4 1.4 %collective-permute-start.3 = (f32[16,2048]{1,0:T(8,128)S(1)}, f32[16,2048]{1,0:T(8,128)S(1)}, u32[]{:S(2)}, u32[]{:S(2)}) collective-permute-start(f32[16,2048]{1,0:T(8,128)S(1)} %collective-permute-done.refs_0_), channel_id=1, source_target_pairs={{0,6},{1,7},{2,0},{3,1},{4,2},{5,3},{6,4},{7,5},{8,14},{9,15},{10,... | collective-permute-start | bytes 393224 | tf_op jit(solution)/shard_map/ppermute | solution.py:110
  17.8 0.0 collective-permute-done.12.refs_5_
  17.8 3.4 %collective-permute-start.14 = (f32[16,2048]{1,0:T(8,128)S(1)}, f32[16,2048]{1,0:T(8,128)S(1)}, u32[]{:S(2)}, u32[]{:S(2)}) collective-permute-start(f32[16,2048]{1,0:T(8,128)S(1)} %collective-permute-done.10.refs_3_), channel_id=1, source_target_pairs={{0,1},{1,0},{2,3},{3,2},{4,5},{5,4},{6,7},{7,6},{8,9},{9,8},{10,11... | collective-permute-start | bytes 393224 | tf_op jit(solution)/shard_map/ppermute | solution.py:110
  21.2 0.0 collective-permute-done.13.refs_6_
  21.2 0.1 collective-permute-start.4
  21.3 0.0 collective-permute-done.1.refs_1_
  21.3 4.0 %collective-permute-start.5 = (f32[16,2048]{1,0:T(8,128)S(1)}, f32[16,2048]{1,0:T(8,128)S(1)}, u32[]{:S(2)}, u32[]{:S(2)}) collective-permute-start(f32[16,2048]{1,0:T(8,128)S(1)} %collective-permute-done.1.refs_1_), channel_id=1, source_target_pairs={{0,1},{1,0},{2,3},{3,2},{4,5},{5,4},{6,7},{7,6},{8,9},{9,8},{10,11... | collective-permute-start | bytes 393224 | tf_op jit(solution)/shard_map/ppermute | solution.py:110
  25.4 0.0 collective-permute-done.2.refs_2_
  25.4 0.0 collective-permute-start.6
  25.4 0.0 collective-permute-done.3.refs_3_
  25.4 0.9 %collective-permute-start.7 = (f32[16,2048]{1,0:T(8,128)S(1)}, f32[16,2048]{1,0:T(8,128)S(1)}, u32[]{:S(2)}, u32[]{:S(2)}) collective-permute-start(f32[16,2048]{1,0:T(8,128)S(1)} %collective-permute-done.3.refs_3_), channel_id=1, source_target_pairs={{0,1},{1,0},{2,3},{3,2},{4,5},{5,4},{6,7},{7,6},{8,9},{9,8},{10,11... | collective-permute-start | bytes 393224 | tf_op jit(solution)/shard_map/ppermute | solution.py:110
  26.3 0.0 copy-start
  26.3 1.6 %copy-done = f32[2048,256]{1,0:T(8,128)S(1)} copy-done((f32[2048,256]{1,0:T(8,128)S(1)}, f32[2048,256]{1,0:T(8,128)}, u32[]{:S(2)}) %copy-start) | copy-done | bytes 2097176
  27.9 0.0 copy-start.2
  27.9 0.8 %copy-done.2 = s32[4096,2]{0,1:T(2,128)S(1)} copy-done((s32[4096,2]{0,1:T(2,128)S(1)}, s32[4096,2]{0,1:T(2,128)}, u32[]{:S(2)}) %copy-start.2) | copy-done | bytes 32792
  28.6 0.0 copy-start.4
  28.6 0.7 %copy-done.4 = f32[512]{0:T(512)S(1)} copy-done((f32[512]{0:T(512)S(1)}, f32[512]{0:T(512)}, u32[]{:S(2)}) %copy-start.4) | copy-done | bytes 2072
  29.3 0.0 copy-start.5
  29.3 0.7 %copy-done.5 = s32[256,2]{0,1:T(2,128)S(1)} copy-done((s32[256,2]{0,1:T(2,128)S(1)}, s32[256,2]{0,1:T(2,128)}, u32[]{:S(2)}) %copy-start.5) | copy-done | bytes 2072
  30.0 0.0 copy-start.6
  30.0 0.7 %copy-done.6 = f32[64]{0:T(128)S(1)} copy-done((f32[64]{0:T(128)S(1)}, f32[64]{0:T(128)}, u32[]{:S(2)}) %copy-start.6) | copy-done | bytes 280
  30.6 0.0 copy-start.1
  30.7 1.4 %shard_map.73 = (f32[32,128]{1,0:T(8,128)S(1)}, bf16[2048,256]{1,0:T(8,128)(2,1)S(1)}, bf16[2048,256]{1,0:T(8,128)(2,1)S(1)}) custom-call(f32[4,128]{1,0:T(4,128)S(1)} %bitcast.11, s32[2,4096]{1,0:T(2,128)S(1)} %bitcast.9, f32[64]{0:T(128)S(1)} %copy-done.6, s32[2,256]{1,0:T(2,128)S(1)} %bitcast.12, f32[2048,256]{1,0:T(8,128)S(1)} %copy-done), custom_call_target="tpu_custom_call" | custom-call | tf_op jit(solution)/shard_map/pallas_call | solution.py:118
  32.1 0.0 collective-permute-done.14.refs_7_
  32.1 0.0 copy-done.1
  32.1 0.6 shard_map.74.refs_10_
  32.7 0.0 copy-start.3
  32.7 0.0 collective-permute-done.4.refs_4_
  32.7 0.0 collective-permute-done.5.refs_5_
  32.7 0.0 collective-permute-done.6.refs_6_
  32.8 0.0 collective-permute-done.7.refs_7_
  32.8 0.6 shard_map.75
  33.4 28.4 %all_to_all.5 = f32[256,2,128]{2,1,0:T(2,128)S(1)} all-to-all(f32[256,2,128]{2,1,0:T(2,128)S(1)} %bitcast.7), channel_id=1, replica_groups=mesh['row'=16,'col'=16] {'row','col'}, dimensions={0} | all-to-all | bytes 524288 | tf_op jit(solution)/shard_map/all_to_all | solution.py:153
  61.7 0.0 copy-done.3
  61.7 0.8 %shard_map.76 = f32[32,128]{1,0:T(8,128)} custom-call(f32[512,128]{1,0:T(8,128)S(1)} %bitcast.8, s32[32,128]{1,0:T(8,128)S(1)} %bitcast.10, f32[32,128]{1,0:T(8,128)S(1)} %get-tuple-element.10.denom_ref), custom_call_target="tpu_custom_call" | custom-call | tf_op jit(solution)/shard_map/pallas_call | solution.py:156
Async XLA Ops:
  0.0 14.3 %collective-permute-start.8 = (f32[16,2048]{1,0:T(8,128)}, f32[16,2048]{1,0:T(8,128)S(1)}, u32[]{:S(2)}, u32[]{:S(2)}) collective-permute-start(f32[16,2048]{1,0:T(8,128)} %refs_0_.1), channel_id=1, source_target_pairs={{0,2},{1,3},{2,4},{3,5},{4,6},{5,7},{6,0},{7,1},{8,10},{9,11},{10,... | collective-permute-start | bytes 393224 | tf_op jit(solution)/shard_map/ppermute | solution.py:110
  2.0 12.3 %collective-permute-start.9 = (f32[16,2048]{1,0:T(8,128)}, f32[16,2048]{1,0:T(8,128)S(1)}, u32[]{:S(2)}, u32[]{:S(2)}) collective-permute-start(f32[16,2048]{1,0:T(8,128)} %refs_0_.1), channel_id=1, source_target_pairs={{0,4},{1,5},{2,6},{3,7},{4,0},{5,1},{6,2},{7,3},{8,12},{9,13},{10,... | collective-permute-start | bytes 393224 | tf_op jit(solution)/shard_map/ppermute | solution.py:110
  4.5 10.4 %collective-permute-start = (f32[16,2048]{1,0:T(8,128)}, f32[16,2048]{1,0:T(8,128)S(1)}, u32[]{:S(2)}, u32[]{:S(2)}) collective-permute-start(f32[16,2048]{1,0:T(8,128)} %refs_0_.1), channel_id=1, source_target_pairs={{0,8},{1,9},{2,10},{3,11},{4,12},{5,13},{6,14},{7,15},{8,0},{9,1},... | collective-permute-start | bytes 393224 | tf_op jit(solution)/shard_map/ppermute | solution.py:110
  11.4 4.3 %collective-permute-start.10 = (f32[16,2048]{1,0:T(8,128)}, f32[16,2048]{1,0:T(8,128)S(1)}, u32[]{:S(2)}, u32[]{:S(2)}) collective-permute-start(f32[16,2048]{1,0:T(8,128)} %refs_0_.1), channel_id=1, source_target_pairs={{0,6},{1,7},{2,0},{3,1},{4,2},{5,3},{6,4},{7,5},{8,14},{9,15},{10,... | collective-permute-start | bytes 393224 | tf_op jit(solution)/shard_map/ppermute | solution.py:110
  12.5 3.9 %collective-permute-start.11 = (f32[16,2048]{1,0:T(8,128)}, f32[16,2048]{1,0:T(8,128)S(1)}, u32[]{:S(2)}, u32[]{:S(2)}) collective-permute-start(f32[16,2048]{1,0:T(8,128)} %refs_0_.1), channel_id=1, source_target_pairs={{0,1},{1,0},{2,3},{3,2},{4,5},{5,4},{6,7},{7,6},{8,9},{9,8},{10,11... | collective-permute-start | bytes 393224 | tf_op jit(solution)/shard_map/ppermute | solution.py:110
  14.3 3.5 %collective-permute-start.12 = (f32[16,2048]{1,0:T(8,128)S(1)}, f32[16,2048]{1,0:T(8,128)S(1)}, u32[]{:S(2)}, u32[]{:S(2)}) collective-permute-start(f32[16,2048]{1,0:T(8,128)S(1)} %collective-permute-done.8.refs_1_), channel_id=1, source_target_pairs={{0,1},{1,0},{2,3},{3,2},{4,5},{5,4},{6,7},{7,6},{8,9},{9,8},{10,11... | collective-permute-start | bytes 393224 | tf_op jit(solution)/shard_map/ppermute | solution.py:110
  14.4 6.9 %collective-permute-start.13 = (f32[16,2048]{1,0:T(8,128)S(1)}, f32[16,2048]{1,0:T(8,128)S(1)}, u32[]{:S(2)}, u32[]{:S(2)}) collective-permute-start(f32[16,2048]{1,0:T(8,128)S(1)} %collective-permute-done.9.refs_2_), channel_id=1, source_target_pairs={{0,1},{1,0},{2,3},{3,2},{4,5},{5,4},{6,7},{7,6},{8,9},{9,8},{10,11... | collective-permute-start | bytes 393224 | tf_op jit(solution)/shard_map/ppermute | solution.py:110
  14.9 6.5 %collective-permute-start.1 = (f32[16,2048]{1,0:T(8,128)S(1)}, f32[16,2048]{1,0:T(8,128)S(1)}, u32[]{:S(2)}, u32[]{:S(2)}) collective-permute-start(f32[16,2048]{1,0:T(8,128)S(1)} %collective-permute-done.refs_0_), channel_id=1, source_target_pairs={{0,2},{1,3},{2,4},{3,5},{4,6},{5,7},{6,0},{7,1},{8,10},{9,11},{10,... | collective-permute-start | bytes 393224 | tf_op jit(solution)/shard_map/ppermute | solution.py:110
  15.7 9.7 %collective-permute-start.2 = (f32[16,2048]{1,0:T(8,128)S(1)}, f32[16,2048]{1,0:T(8,128)S(1)}, u32[]{:S(2)}, u32[]{:S(2)}) collective-permute-start(f32[16,2048]{1,0:T(8,128)S(1)} %collective-permute-done.refs_0_), channel_id=1, source_target_pairs={{0,4},{1,5},{2,6},{3,7},{4,0},{5,1},{6,2},{7,3},{8,12},{9,13},{10,... | collective-permute-start | bytes 393224 | tf_op jit(solution)/shard_map/ppermute | solution.py:110
  16.4 8.9 %collective-permute-start.3 = (f32[16,2048]{1,0:T(8,128)S(1)}, f32[16,2048]{1,0:T(8,128)S(1)}, u32[]{:S(2)}, u32[]{:S(2)}) collective-permute-start(f32[16,2048]{1,0:T(8,128)S(1)} %collective-permute-done.refs_0_), channel_id=1, source_target_pairs={{0,6},{1,7},{2,0},{3,1},{4,2},{5,3},{6,4},{7,5},{8,14},{9,15},{10,... | collective-permute-start | bytes 393224 | tf_op jit(solution)/shard_map/ppermute | solution.py:110
  17.8 14.3 %collective-permute-start.14 = (f32[16,2048]{1,0:T(8,128)S(1)}, f32[16,2048]{1,0:T(8,128)S(1)}, u32[]{:S(2)}, u32[]{:S(2)}) collective-permute-start(f32[16,2048]{1,0:T(8,128)S(1)} %collective-permute-done.10.refs_3_), channel_id=1, source_target_pairs={{0,1},{1,0},{2,3},{3,2},{4,5},{5,4},{6,7},{7,6},{8,9},{9,8},{10,11... | collective-permute-start | bytes 393224 | tf_op jit(solution)/shard_map/ppermute | solution.py:110
  21.2 11.5 %collective-permute-start.4 = (f32[16,2048]{1,0:T(8,128)S(1)}, f32[16,2048]{1,0:T(8,128)S(1)}, u32[]{:S(2)}, u32[]{:S(2)}) collective-permute-start(f32[16,2048]{1,0:T(8,128)S(1)} %collective-permute-done.refs_0_), channel_id=1, source_target_pairs={{0,1},{1,0},{2,3},{3,2},{4,5},{5,4},{6,7},{7,6},{8,9},{9,8},{10,11... | collective-permute-start | bytes 393224 | tf_op jit(solution)/shard_map/ppermute | solution.py:110
  21.3 11.4 %collective-permute-start.5 = (f32[16,2048]{1,0:T(8,128)S(1)}, f32[16,2048]{1,0:T(8,128)S(1)}, u32[]{:S(2)}, u32[]{:S(2)}) collective-permute-start(f32[16,2048]{1,0:T(8,128)S(1)} %collective-permute-done.1.refs_1_), channel_id=1, source_target_pairs={{0,1},{1,0},{2,3},{3,2},{4,5},{5,4},{6,7},{7,6},{8,9},{9,8},{10,11... | collective-permute-start | bytes 393224 | tf_op jit(solution)/shard_map/ppermute | solution.py:110
  25.4 7.4 %collective-permute-start.6 = (f32[16,2048]{1,0:T(8,128)S(1)}, f32[16,2048]{1,0:T(8,128)S(1)}, u32[]{:S(2)}, u32[]{:S(2)}) collective-permute-start(f32[16,2048]{1,0:T(8,128)S(1)} %collective-permute-done.2.refs_2_), channel_id=1, source_target_pairs={{0,1},{1,0},{2,3},{3,2},{4,5},{5,4},{6,7},{7,6},{8,9},{9,8},{10,11... | collective-permute-start | bytes 393224 | tf_op jit(solution)/shard_map/ppermute | solution.py:110
  25.4 7.4 %collective-permute-start.7 = (f32[16,2048]{1,0:T(8,128)S(1)}, f32[16,2048]{1,0:T(8,128)S(1)}, u32[]{:S(2)}, u32[]{:S(2)}) collective-permute-start(f32[16,2048]{1,0:T(8,128)S(1)} %collective-permute-done.3.refs_3_), channel_id=1, source_target_pairs={{0,1},{1,0},{2,3},{3,2},{4,5},{5,4},{6,7},{7,6},{8,9},{9,8},{10,11... | collective-permute-start | bytes 393224 | tf_op jit(solution)/shard_map/ppermute | solution.py:110
  26.3 1.6 %copy-start = (f32[2048,256]{1,0:T(8,128)S(1)}, f32[2048,256]{1,0:T(8,128)}, u32[]{:S(2)}) copy-start(f32[2048,256]{1,0:T(8,128)} %b_ref.1) | copy-start | bytes 6291460
  27.9 0.8 %copy-start.2 = (s32[4096,2]{0,1:T(2,128)S(1)}, s32[4096,2]{0,1:T(2,128)}, u32[]{:S(2)}) copy-start(s32[4096,2]{0,1:T(2,128)} %param.13) | copy-start | bytes 98308
  28.6 0.7 %copy-start.4 = (f32[512]{0:T(512)S(1)}, f32[512]{0:T(512)}, u32[]{:S(2)}) copy-start(f32[512]{0:T(512)} %param.11) | copy-start | bytes 6148
  29.3 0.7 %copy-start.5 = (s32[256,2]{0,1:T(2,128)S(1)}, s32[256,2]{0,1:T(2,128)}, u32[]{:S(2)}) copy-start(s32[256,2]{0,1:T(2,128)} %param.12) | copy-start | bytes 6148
  30.0 0.7 %copy-start.6 = (f32[64]{0:T(128)S(1)}, f32[64]{0:T(128)}, u32[]{:S(2)}) copy-start(f32[64]{0:T(128)} %occ_ref.1) | copy-start | bytes 772
  30.6 1.5 %copy-start.1 = (f32[16,2048]{1,0:T(8,128)S(1)}, f32[16,2048]{1,0:T(8,128)}, u32[]{:S(2)}) copy-start(f32[16,2048]{1,0:T(8,128)} %refs_0_.1) | copy-start | bytes 393220
  32.7 29.0 %copy-start.3 = (s32[4096]{0:T(1024)S(1)}, s32[4096]{0:T(1024)}, u32[]{:S(2)}) copy-start(s32[4096]{0:T(1024)} %param.9) | copy-start | bytes 49156

commit v3 on v2

--- a/solution.py
+++ b/solution.py
@@ -5,7 +5,7 @@
 from jax.experimental.pallas import tpu as pltpu
 from jax.sharding import PartitionSpec as P
 
-X, CORES, LANES = 4, 2, 128
+X, CORES, LANES, PIECES = 4, 2, 128, 4
 VMEM = pltpu.VMEM
 SMEM = pltpu.SMEM
 LIMIT = pltpu.CompilerParams(vmem_limit_bytes=24 << 20)
@@ -13,6 +13,11 @@
 
 def place(z, x, core):
     return (z * X + x % X) * CORES + core
+
+
+def position():
+    me = lax.axis_index("col")
+    return me // (X * CORES), (me // CORES) % X, me % CORES
 
 
 def shift(dz=0, dx=0, dcore=0):
@@ -39,14 +44,60 @@
     return high, (value - high.astype(jnp.float32)).astype(jnp.bfloat16)
 
 
-def prepare(virt_ref, col_ref, occ_ref, row_ref, b_ref, denom_ref, high_ref, low_ref):
-    high_ref[...], low_ref[...] = halves(b_ref[...])
+def choose(own_ref, other_ref, out_ref):
+    core = position()[2]
+    half = own_ref.shape[0] // CORES
+    line = lax.broadcasted_iota(jnp.int32, (half, LANES), 0)
+    spot = (CORES * line + core) % half
+    for ref, at in ((own_ref, core), (other_ref, 1 - core)):
+        for k in range(0, ref.shape[1], LANES):
+            upper, lower = (
+                jnp.take_along_axis(
+                    ref[h : h + half, k : k + LANES], spot, axis=0, mode="promise_in_bounds"
+                )
+                for h in (0, half)
+            )
+            chosen = jnp.where(line < half // CORES, upper, lower)
+            out_ref[pl.ds(pl.multiple_of(at * half, half), half), k : k + LANES] = chosen
+
+
+def stage(block_ref, out_ref, sem):
+    copy = pltpu.make_async_copy(block_ref, out_ref, sem)
+    copy.start()
+    copy.wait()
+
+
+def prepare(
+    virt_ref, col_ref, occ_ref, row_ref, b_ref, other_ref,
+    denom_ref, high_ref, low_ref,
+    virt, cols, occ, rows, b, sems, b_sems,
+):
+    copies = [
+        pltpu.make_async_copy(source, target, sems.at[k])
+        for k, (source, target) in enumerate(
+            ((virt_ref, virt), (col_ref, cols), (occ_ref, occ), (row_ref, rows))
+        )
+    ]
+    step = b.shape[0] // PIECES
+    pieces = [pl.ds(k * step, step) for k in range(PIECES)]
+    b_copies = [
+        pltpu.make_async_copy(b_ref.at[piece], b.at[piece], b_sems.at[k])
+        for k, piece in enumerate(pieces)
+    ]
+    for copy in copies + b_copies:
+        copy.start()
+    for copy in copies:
+        copy.wait()
     me = lax.axis_index("row") * lax.axis_size("col") + lax.axis_index("col")
-    row_part = occ_ref[row_ref[0, me]] + occ_ref[row_ref[1, me]]
+    row_part = occ[rows[0, me]] + occ[rows[1, me]]
     for k in range(denom_ref.shape[0]):
-        lanes = slice(k * LANES, (k + 1) * LANES)
-        pair = lookup(virt_ref[...], col_ref[:, lanes])
+        pair = lookup(virt[...], cols[:, k * LANES : (k + 1) * LANES])
         denom_ref[k : k + 1] = row_part - (pair[:1] + pair[1:])
+    width = b.shape[1]
+    for copy, piece in zip(b_copies, pieces):
+        copy.wait()
+        high_ref[piece, :width], low_ref[piece, :width] = halves(b[piece, :])
+    high_ref[:, width:], low_ref[:, width:] = halves(other_ref[...])
 
 
 def product(block_refs, high_ref, low_ref, a_ref):
@@ -70,14 +121,15 @@
     *blocks, high_ref, low_ref, near_ref, out_ref, a_ref, done_ref = refs
     rows = blocks[0].shape[0]
     done_ref[...] = product(blocks, high_ref, low_ref, a_ref)
-    me = lax.axis_index("col")
-    z, x, core = me // (X * CORES), (me // CORES) % X, me % CORES
+    z, x, core = position()
+    each = done_ref.shape[1] // LANES
     for ref, dz in ((near_ref, 0), (done_ref, 1)):
-        for k in range(len(blocks)):
-            source = place(z ^ dz, x + X - k % X, core ^ (k // X))
-            for h in range(2):
-                out_ref[pl.ds(source * (2 * rows) + h, rows, stride=2), :] = ref[
-                    k * rows : (k + 1) * rows, h * LANES : (h + 1) * LANES
+        for k in range(X):
+            first = place(z ^ dz, x + X - k, 0) // CORES * (rows * each)
+            for q in range(each):
+                to = (core ^ (q // (each // CORES))) * (each // CORES) + q % (each // CORES)
+                out_ref[pl.ds(first + to, rows, stride=each), :] = ref[
+                    k * rows : (k + 1) * rows, q * LANES : (q + 1) * LANES
                 ]
 
 
@@ -97,11 +149,11 @@
 ):
     rows, depth = lambda_amps.shape
     window = exchanged.shape[0]
-    width = cycle_inter.shape[1]
+    wide = (depth, CORES * cycle_inter.shape[1])
     lines = window // LANES
-    count = X * CORES
-    v, s = pl.BlockSpec(memory_space=VMEM), pl.BlockSpec(memory_space=SMEM)
-    split = VMEM((2 * count * rows, depth), jnp.bfloat16)
+    v, anywhere = pl.BlockSpec(memory_space=VMEM), pl.BlockSpec(memory_space=pl.ANY)
+    split = VMEM((2 * X * rows, depth), jnp.bfloat16)
+    part = VMEM((X * rows, wide[1]), jnp.float32)
 
     def here(value):
         return pltpu.with_memory_space_constraint(value, VMEM)
@@ -109,49 +161,86 @@
     def send(block, **by):
         return lax.ppermute(block, "col", shift(**by))
 
-    def spread(block):
-        line = [block] + [send(block, dx=k) for k in (1, 2, 3)]
-        return line + [send(part, dcore=1) for part in line]
-
-    swapped = send(lambda_amps, dz=1)
-    near_blocks = spread(lambda_amps)
+    def spread(block, *steps):
+        return {k: send(block, dx=k) for k in steps}
+
+    other = send(lambda_amps, dcore=1)
+    own = pl.pallas_call(
+        stage,
+        out_shape=VMEM(lambda_amps.shape, jnp.float32),
+        in_specs=[anywhere],
+        out_specs=v,
+        scratch_shapes=[pltpu.SemaphoreType.DMA],
+        compiler_params=LIMIT,
+    )(pltpu.with_memory_space_constraint(lambda_amps, pltpu.HBM))
+    block = pl.pallas_call(
+        choose,
+        out_shape=VMEM(lambda_amps.shape, jnp.float32),
+        in_specs=[v, v],
+        out_specs=v,
+        compiler_params=LIMIT,
+    )(here(own), here(other))
+    swapped = send(block, dz=1)
+    other_inter = send(cycle_inter, dcore=1)
+    near_blocks = {0: block, **spread(block, 1, 2, 3)}
     denom, high, low = pl.pallas_call(
         prepare,
         out_shape=(
             VMEM((lines, LANES), jnp.float32),
-            VMEM(cycle_inter.shape, jnp.bfloat16),
-            VMEM(cycle_inter.shape, jnp.bfloat16),
+            VMEM(wide, jnp.bfloat16),
+            VMEM(wide, jnp.bfloat16),
         ),
-        in_specs=[v, v, s, s, v],
+        in_specs=[anywhere] * 5 + [v],
         out_specs=(v, v, v),
+        scratch_shapes=[
+            VMEM((virt_energy.shape[0] // LANES, LANES), jnp.float32),
+            VMEM((2, window), jnp.int32),
+            SMEM(occ_energy.shape, jnp.float32),
+            SMEM((2, row_orbitals.shape[0]), jnp.int32),
+            VMEM(cycle_inter.shape, jnp.float32),
+            pltpu.SemaphoreType.DMA((4,)),
+            pltpu.SemaphoreType.DMA((PIECES,)),
+        ],
         compiler_params=LIMIT,
     )(
-        virt_energy.reshape(-1, LANES),
-        col_orbitals.T,
-        occ_energy,
-        row_orbitals.T,
-        here(cycle_inter),
+        *(
+            pltpu.with_memory_space_constraint(value, pltpu.HBM)
+            for value in (
+                virt_energy.reshape(-1, LANES),
+                col_orbitals.T,
+                occ_energy,
+                row_orbitals.T,
+                cycle_inter,
+            )
+        ),
+        here(other_inter),
     )
     near_part = pl.pallas_call(
         near,
-        out_shape=VMEM((count * rows, width), jnp.float32),
-        in_specs=[v] * (count + 2),
+        out_shape=part,
+        in_specs=[v] * (X + 2),
         out_specs=v,
         scratch_shapes=[split],
         compiler_params=LIMIT,
-    )(*map(here, near_blocks), here(high), here(low))
-    far_blocks = spread(swapped)
+    )(*(here(near_blocks[k]) for k in range(X)), here(high), here(low))
+    far_blocks = {0: swapped, **spread(swapped, 1, 2, 3)}
+    owners = lax.axis_size("row") * lax.axis_size("col")
+    each = wide[1] // LANES
     parts = pl.pallas_call(
         far,
-        out_shape=VMEM((4 * count * rows, LANES), jnp.float32),
-        in_specs=[v] * (count + 3),
-        out_specs=v,
-        scratch_shapes=[split, VMEM((count * rows, width), jnp.float32)],
-        compiler_params=LIMIT,
-    )(*map(here, far_blocks), here(high), here(low), here(near_part))
-    owners = lax.axis_size("row") * lax.axis_size("col")
+        out_shape=VMEM((owners // CORES * each, LANES), jnp.float32),
+        in_specs=[v] * (X + 3),
+        out_specs=v,
+        scratch_shapes=[split, part],
+        compiler_params=LIMIT,
+    )(*(here(far_blocks[k]) for k in range(X)), here(high), here(low), here(near_part))
     parts = lax.all_to_all(
-        parts.reshape(owners, -1, LANES), ("row", "col"), 0, 0, tiled=True
+        parts.reshape(-1, each, LANES),
+        ("row", "col"),
+        0,
+        0,
+        tiled=True,
+        axis_index_groups=[list(range(core, owners, CORES)) for core in range(CORES)],
     )
     update = pl.pallas_call(
         finish,

time: 62.9 us -> 55.2 us (0.88)
  the two profiles are of different devices: /device:TPU:1 before, /device:TPU:32 now
where the time goes in v3:
time: 55.2 us; the launch traced here: 55.1 us
  blocking collectives  25.9 us (47%)
  starting transfers between devices  18.2 us (33%)
  waiting for transfers between devices  5.56 us (10%)
  Pallas kernels  5.35 us (10%)
    all_to_all x1, blocking collectives, shards(): lax.all_to_all(parts.reshape(-1, each, LANES), ('row', 'col'), 0, 0, tile...  25.9 us
    ppermute x9, starting transfers between devices, send(): return lax.ppermute(block, 'col', shift(**by))  18.2 us
    ppermute x9, waiting for transfers between devices, send(): return lax.ppermute(block, 'col', shift(**by))  5.56 us
    pallas_call x1, Pallas kernels, shards(): pl.pallas_call(prepare, out_shape=(VMEM((lines, LANES), jnp.float32), VME...  2.02 us
  transfers between devices with their start and end apart: 9, of which 3 were waited for; matrix products, arithmetic and copies ran while one was open for 0% of the time, Pallas kernels for 7%

profile of v3, /device:TPU:32, one launch (start us, length us, event | category | flops | bytes accessed | tf_op | source)
XLA Modules:
  0.0 55.1 jit_solution(10859450982777994299)
XLA Ops:
  0.0 0.0 collective-permute-start.5
  0.0 0.5 collective-permute-start
  0.5 0.9 %shard_map.73.own_ref = f32[16,2048]{1,0:T(8,128)S(1)} custom-call(f32[16,2048]{1,0:T(8,128)} %block_ref.1), custom_call_target="tpu_custom_call" | custom-call | tf_op jit(solution)/shard_map/pallas_call | solution.py:168
  1.4 3.1 %collective-permute-done.other_ref = f32[16,2048]{1,0:T(8,128)S(1)} collective-permute-done((f32[16,2048]{1,0:T(8,128)}, f32[16,2048]{1,0:T(8,128)S(1)}, u32[]{:S(2)}, u32[]{:S(2)}) %collective-permute-start) | collective-permute-done | bytes 131104 | tf_op jit(solution)/shard_map/ppermute | solution.py:162
  4.6 6.4 %collective-permute-start.1 = (f32[16,2048]{1,0:T(8,128)S(1)}, f32[16,2048]{1,0:T(8,128)S(1)}, u32[]{:S(2)}, u32[]{:S(2)}) collective-permute-start(f32[16,2048]{1,0:T(8,128)S(1)} %shard_map.74.refs_0_), channel_id=1, source_target_pairs={{0,8},{1,9},{2,10},{3,11},{4,12},{5,13},{6,14},{7,15},{8,0},{9,1},... | collective-permute-start | bytes 393224 | tf_op jit(solution)/shard_map/ppermute | solution.py:162
  11.0 1.5 %collective-permute-start.6 = (f32[16,2048]{1,0:T(8,128)S(1)}, f32[16,2048]{1,0:T(8,128)S(1)}, u32[]{:S(2)}, u32[]{:S(2)}) collective-permute-start(f32[16,2048]{1,0:T(8,128)S(1)} %shard_map.74.refs_0_), channel_id=1, source_target_pairs={{0,2},{1,3},{2,4},{3,5},{4,6},{5,7},{6,0},{7,1},{8,10},{9,11},{10,... | collective-permute-start | bytes 393224 | tf_op jit(solution)/shard_map/ppermute | solution.py:162
  12.5 2.7 %collective-permute-start.7 = (f32[16,2048]{1,0:T(8,128)S(1)}, f32[16,2048]{1,0:T(8,128)S(1)}, u32[]{:S(2)}, u32[]{:S(2)}) collective-permute-start(f32[16,2048]{1,0:T(8,128)S(1)} %shard_map.74.refs_0_), channel_id=1, source_target_pairs={{0,4},{1,5},{2,6},{3,7},{4,0},{5,1},{6,2},{7,3},{8,12},{9,13},{10,... | collective-permute-start | bytes 393224 | tf_op jit(solution)/shard_map/ppermute | solution.py:162
  15.2 1.4 %collective-permute-start.8 = (f32[16,2048]{1,0:T(8,128)S(1)}, f32[16,2048]{1,0:T(8,128)S(1)}, u32[]{:S(2)}, u32[]{:S(2)}) collective-permute-start(f32[16,2048]{1,0:T(8,128)S(1)} %shard_map.74.refs_0_), channel_id=1, source_target_pairs={{0,6},{1,7},{2,0},{3,1},{4,2},{5,3},{6,4},{7,5},{8,14},{9,15},{10,... | collective-permute-start | bytes 393224 | tf_op jit(solution)/shard_map/ppermute | solution.py:162
  16.6 1.0 %collective-permute-done.1.refs_0_ = f32[16,2048]{1,0:T(8,128)S(1)} collective-permute-done((f32[16,2048]{1,0:T(8,128)S(1)}, f32[16,2048]{1,0:T(8,128)S(1)}, u32[]{:S(2)}, u32[]{:S(2)}) %collective-permute-start.1) | collective-permute-done | bytes 131104 | tf_op jit(solution)/shard_map/ppermute | solution.py:162
  17.6 1.5 %collective-permute-start.2 = (f32[16,2048]{1,0:T(8,128)S(1)}, f32[16,2048]{1,0:T(8,128)S(1)}, u32[]{:S(2)}, u32[]{:S(2)}) collective-permute-start(f32[16,2048]{1,0:T(8,128)S(1)} %collective-permute-done.1.refs_0_), channel_id=1, source_target_pairs={{0,2},{1,3},{2,4},{3,5},{4,6},{5,7},{6,0},{7,1},{8,10},{9,11},{10,... | collective-permute-start | bytes 393224 | tf_op jit(solution)/shard_map/ppermute | solution.py:162
  19.1 0.0 collective-permute-done.6.refs_1_
  19.1 2.7 %collective-permute-start.3 = (f32[16,2048]{1,0:T(8,128)S(1)}, f32[16,2048]{1,0:T(8,128)S(1)}, u32[]{:S(2)}, u32[]{:S(2)}) collective-permute-start(f32[16,2048]{1,0:T(8,128)S(1)} %collective-permute-done.1.refs_0_), channel_id=1, source_target_pairs={{0,4},{1,5},{2,6},{3,7},{4,0},{5,1},{6,2},{7,3},{8,12},{9,13},{10,... | collective-permute-start | bytes 393224 | tf_op jit(solution)/shard_map/ppermute | solution.py:162
  21.9 0.0 collective-permute-done.5.other_ref
  21.9 1.4 %collective-permute-start.4 = (f32[16,2048]{1,0:T(8,128)S(1)}, f32[16,2048]{1,0:T(8,128)S(1)}, u32[]{:S(2)}, u32[]{:S(2)}) collective-permute-start(f32[16,2048]{1,0:T(8,128)S(1)} %collective-permute-done.1.refs_0_), channel_id=1, source_target_pairs={{0,6},{1,7},{2,0},{3,1},{4,2},{5,3},{6,4},{7,5},{8,14},{9,15},{10,... | collective-permute-start | bytes 393224 | tf_op jit(solution)/shard_map/ppermute | solution.py:162
  23.3 2.0 %shard_map.75 = (f32[32,128]{1,0:T(8,128)S(1)}, bf16[2048,512]{1,0:T(8,128)(2,1)S(1)}, bf16[2048,512]{1,0:T(8,128)(2,1)S(1)}) custom-call(f32[4,128]{1,0:T(4,128)} %bitcast.11, s32[2,4096]{1,0:T(2,128)} %bitcast.10, f32[64]{0:T(128)} %occ_ref.1, s32[2,256]{1,0:T(2,128)} %bitcast.12, f32[2048,256]{1,0:T(8,128)} %b_ref.1, ...), custom_call_target="tpu_custom_call" | custom-call | tf_op jit(solution)/shard_map/pallas_call | solution.py:186
  25.3 0.0 collective-permute-done.7.refs_2_
  25.3 0.0 collective-permute-done.8.refs_3_
  25.3 0.8 %shard_map.76.refs_6_ = f32[64,512]{1,0:T(8,128)S(1)} custom-call(f32[16,2048]{1,0:T(8,128)S(1)} %shard_map.74.refs_0_, f32[16,2048]{1,0:T(8,128)S(1)} %collective-permute-done.6.refs_1_, f32[16,2048]{1,0:T(8,128)S(1)} %collective-permute-done.7.refs_2_, f32[16,2048]{1,0:T(8,128)S(1)} %collective-permute-done.8.refs_3_, ...), custom_call_target="tpu_custom_call" | custom-call | tf_op jit(solution)/shard_map/pallas_call | solution.py:218
  26.1 0.0 copy-start
  26.1 0.0 collective-permute-done.2.refs_1_
  26.1 1.4 %collective-permute-done.3.refs_2_ = f32[16,2048]{1,0:T(8,128)S(1)} collective-permute-done((f32[16,2048]{1,0:T(8,128)S(1)}, f32[16,2048]{1,0:T(8,128)S(1)}, u32[]{:S(2)}, u32[]{:S(2)}) %collective-permute-start.3) | collective-permute-done | bytes 131104 | tf_op jit(solution)/shard_map/ppermute | solution.py:162
  27.5 0.0 collective-permute-done.4.refs_3_
  27.6 0.8 %shard_map.77 = f32[512,128]{1,0:T(8,128)S(1)} custom-call(f32[16,2048]{1,0:T(8,128)S(1)} %collective-permute-done.1.refs_0_, f32[16,2048]{1,0:T(8,128)S(1)} %collective-permute-done.2.refs_1_, f32[16,2048]{1,0:T(8,128)S(1)} %collective-permute-done.3.refs_2_, f32[16,2048]{1,0:T(8,128)S(1)} %collective-permute-done.4.refs_3_, ...), custom_call_target="tpu_custom_call" | custom-call | tf_op jit(solution)/shard_map/pallas_call | solution.py:229
  28.3 25.9 %all_to_all.5 = f32[128,4,128]{2,1,0:T(4,128)S(1)} all-to-all(f32[128,4,128]{2,1,0:T(4,128)S(1)} %bitcast.7), channel_id=1, replica_groups={{0,2,4,6,8,10,12,14,16,18,20,22,24,26,28,30,32,34,36,38,40,42,44,46,48,..., dimensions={0} | all-to-all | bytes 524288 | tf_op jit(solution)/shard_map/all_to_all | solution.py:237
  54.2 0.0 copy-done
  54.2 0.8 %shard_map.78 = f32[32,128]{1,0:T(8,128)} custom-call(f32[512,128]{1,0:T(8,128)S(1)} %bitcast.8, s32[32,128]{1,0:T(8,128)S(1)} %bitcast.9, f32[32,128]{1,0:T(8,128)S(1)} %get-tuple-element.10.denom_ref), custom_call_target="tpu_custom_call" | custom-call | tf_op jit(solution)/shard_map/pallas_call | solution.py:245
  (1 shorter events, 0.0 us)
Async XLA Ops:
  0.0 21.9 %collective-permute-start.5 = (f32[2048,256]{1,0:T(8,128)}, f32[2048,256]{1,0:T(8,128)S(1)}, u32[]{:S(2)}, u32[]{:S(2)}) collective-permute-start(f32[2048,256]{1,0:T(8,128)} %b_ref.1), channel_id=1, source_target_pairs={{0,1},{1,0},{2,3},{3,2},{4,5},{5,4},{6,7},{7,6},{8,9},{9,8},{10,11... | collective-permute-start | bytes 6291464 | tf_op jit(solution)/shard_map/ppermute | solution.py:162
  0.0 4.6 %collective-permute-start = (f32[16,2048]{1,0:T(8,128)}, f32[16,2048]{1,0:T(8,128)S(1)}, u32[]{:S(2)}, u32[]{:S(2)}) collective-permute-start(f32[16,2048]{1,0:T(8,128)} %block_ref.1), channel_id=1, source_target_pairs={{0,1},{1,0},{2,3},{3,2},{4,5},{5,4},{6,7},{7,6},{8,9},{9,8},{10,11... | collective-permute-start | bytes 393224 | tf_op jit(solution)/shard_map/ppermute | solution.py:162
  4.6 13.0 %collective-permute-start.1 = (f32[16,2048]{1,0:T(8,128)S(1)}, f32[16,2048]{1,0:T(8,128)S(1)}, u32[]{:S(2)}, u32[]{:S(2)}) collective-permute-start(f32[16,2048]{1,0:T(8,128)S(1)} %shard_map.74.refs_0_), channel_id=1, source_target_pairs={{0,8},{1,9},{2,10},{3,11},{4,12},{5,13},{6,14},{7,15},{8,0},{9,1},... | collective-permute-start | bytes 393224 | tf_op jit(solution)/shard_map/ppermute | solution.py:162
  11.0 8.1 %collective-permute-start.6 = (f32[16,2048]{1,0:T(8,128)S(1)}, f32[16,2048]{1,0:T(8,128)S(1)}, u32[]{:S(2)}, u32[]{:S(2)}) collective-permute-start(f32[16,2048]{1,0:T(8,128)S(1)} %shard_map.74.refs_0_), channel_id=1, source_target_pairs={{0,2},{1,3},{2,4},{3,5},{4,6},{5,7},{6,0},{7,1},{8,10},{9,11},{10,... | collective-permute-start | bytes 393224 | tf_op jit(solution)/shard_map/ppermute | solution.py:162
  12.5 12.9 %collective-permute-start.7 = (f32[16,2048]{1,0:T(8,128)S(1)}, f32[16,2048]{1,0:T(8,128)S(1)}, u32[]{:S(2)}, u32[]{:S(2)}) collective-permute-start(f32[16,2048]{1,0:T(8,128)S(1)} %shard_map.74.refs_0_), channel_id=1, source_target_pairs={{0,4},{1,5},{2,6},{3,7},{4,0},{5,1},{6,2},{7,3},{8,12},{9,13},{10,... | collective-permute-start | bytes 393224 | tf_op jit(solution)/shard_map/ppermute | solution.py:162
  15.2 10.1 %collective-permute-start.8 = (f32[16,2048]{1,0:T(8,128)S(1)}, f32[16,2048]{1,0:T(8,128)S(1)}, u32[]{:S(2)}, u32[]{:S(2)}) collective-permute-start(f32[16,2048]{1,0:T(8,128)S(1)} %shard_map.74.refs_0_), channel_id=1, source_target_pairs={{0,6},{1,7},{2,0},{3,1},{4,2},{5,3},{6,4},{7,5},{8,14},{9,15},{10,... | collective-permute-start | bytes 393224 | tf_op jit(solution)/shard_map/ppermute | solution.py:162
  17.6 8.5 %collective-permute-start.2 = (f32[16,2048]{1,0:T(8,128)S(1)}, f32[16,2048]{1,0:T(8,128)S(1)}, u32[]{:S(2)}, u32[]{:S(2)}) collective-permute-start(f32[16,2048]{1,0:T(8,128)S(1)} %collective-permute-done.1.refs_0_), channel_id=1, source_target_pairs={{0,2},{1,3},{2,4},{3,5},{4,6},{5,7},{6,0},{7,1},{8,10},{9,11},{10,... | collective-permute-start | bytes 393224 | tf_op jit(solution)/shard_map/ppermute | solution.py:162
  19.1 8.4 %collective-permute-start.3 = (f32[16,2048]{1,0:T(8,128)S(1)}, f32[16,2048]{1,0:T(8,128)S(1)}, u32[]{:S(2)}, u32[]{:S(2)}) collective-permute-start(f32[16,2048]{1,0:T(8,128)S(1)} %collective-permute-done.1.refs_0_), channel_id=1, source_target_pairs={{0,4},{1,5},{2,6},{3,7},{4,0},{5,1},{6,2},{7,3},{8,12},{9,13},{10,... | collective-permute-start | bytes 393224 | tf_op jit(solution)/shard_map/ppermute | solution.py:162
  21.9 5.7 %collective-permute-start.4 = (f32[16,2048]{1,0:T(8,128)S(1)}, f32[16,2048]{1,0:T(8,128)S(1)}, u32[]{:S(2)}, u32[]{:S(2)}) collective-permute-start(f32[16,2048]{1,0:T(8,128)S(1)} %collective-permute-done.1.refs_0_), channel_id=1, source_target_pairs={{0,6},{1,7},{2,0},{3,1},{4,2},{5,3},{6,4},{7,5},{8,14},{9,15},{10,... | collective-permute-start | bytes 393224 | tf_op jit(solution)/shard_map/ppermute | solution.py:162
  26.1 28.1 %copy-start = (s32[4096]{0:T(1024)S(1)}, s32[4096]{0:T(1024)}, u32[]{:S(2)}) copy-start(s32[4096]{0:T(1024)} %param.9) | copy-start | bytes 49156

commit v4 on v3

--- a/solution.py
+++ b/solution.py
@@ -12,7 +12,7 @@
 
 
 def place(z, x, core):
-    return (z * X + x % X) * CORES + core
+    return (z * X + x) * CORES + core
 
 
 def position():
@@ -22,7 +22,7 @@
 
 def shift(dz=0, dx=0, dcore=0):
     return [
-        (place(z, x, core), place(z ^ dz, x + dx, core ^ dcore))
+        (place(z, x, core), place(z ^ dz, x ^ dx, core ^ dcore))
         for z in range(2)
         for x in range(X)
         for core in range(CORES)
@@ -125,7 +125,7 @@
     each = done_ref.shape[1] // LANES
     for ref, dz in ((near_ref, 0), (done_ref, 1)):
         for k in range(X):
-            first = place(z ^ dz, x + X - k, 0) // CORES * (rows * each)
+            first = place(z ^ dz, x ^ k, 0) // CORES * (rows * each)
             for q in range(each):
                 to = (core ^ (q // (each // CORES))) * (each // CORES) + q % (each // CORES)
                 out_ref[pl.ds(first + to, rows, stride=each), :] = ref[
@@ -235,7 +235,7 @@
         compiler_params=LIMIT,
     )(*(here(far_blocks[k]) for k in range(X)), here(high), here(low), here(near_part))
     parts = lax.all_to_all(
-        parts.reshape(-1, each, LANES),
+        parts.reshape(-1, 1, each * LANES),
         ("row", "col"),
         0,
         0,

time: 55.2 us -> 55.7 us (level)
  waiting for transfers between devices: 5.56 us -> 9.49 us
  starting transfers between devices: 18.2 us -> 16.3 us
  blocking collectives: 25.9 us -> 24.4 us
    ppermute x9, waiting for transfers between devices: 5.56 us -> 9.49 us  [send(): return lax.ppermute(block, 'col', shift(**by))]
    ppermute x9, starting transfers between devices: 18.2 us -> 16.3 us  [send(): return lax.ppermute(block, 'col', shift(**by))]
    all_to_all x1, blocking collectives: 25.9 us -> 24.4 us  [shards(): lax.all_to_all(parts.reshape(-1, 1, each * LANES), ('row', 'col'), 0, 0,...]
  transfers between devices with their start and end apart: 9 -> 9, of which waited for: 3 -> 4; matrix products, arithmetic and copies ran while one was open for 0% -> 0% of each run, Pallas kernels for 7% -> 7%
where the time goes in v4:
time: 55.7 us; the launch traced here: 55.5 us
  blocking collectives  24.4 us (44%)
  starting transfers between devices  16.3 us (29%)
  waiting for transfers between devices  9.49 us (17%)
  Pallas kernels  5.34 us (10%)
    all_to_all x1, blocking collectives, shards(): lax.all_to_all(parts.reshape(-1, 1, each * LANES), ('row', 'col'), 0, 0,...  24.4 us
    ppermute x9, starting transfers between devices, send(): return lax.ppermute(block, 'col', shift(**by))  16.3 us
    ppermute x9, waiting for transfers between devices, send(): return lax.ppermute(block, 'col', shift(**by))  9.49 us
    pallas_call x1, Pallas kernels, shards(): pl.pallas_call(prepare, out_shape=(VMEM((lines, LANES), jnp.float32), VME...  2.02 us
  transfers between devices with their start and end apart: 9, of which 4 were waited for; matrix products, arithmetic and copies ran while one was open for 0% of the time, Pallas kernels for 7%

profile of v4, /device:TPU:32, one launch (start us, length us, event | category | flops | bytes accessed | tf_op | source)
XLA Modules:
  0.0 55.5 jit_solution(919145264830864291)
XLA Ops:
  0.0 0.0 collective-permute-start.5
  0.0 0.5 collective-permute-start
  0.5 0.9 %shard_map.73.own_ref = f32[16,2048]{1,0:T(8,128)S(1)} custom-call(f32[16,2048]{1,0:T(8,128)} %block_ref.1), custom_call_target="tpu_custom_call" | custom-call | tf_op jit(solution)/shard_map/pallas_call | solution.py:168
  1.4 3.1 %collective-permute-done.other_ref = f32[16,2048]{1,0:T(8,128)S(1)} collective-permute-done((f32[16,2048]{1,0:T(8,128)}, f32[16,2048]{1,0:T(8,128)S(1)}, u32[]{:S(2)}, u32[]{:S(2)}) %collective-permute-start) | collective-permute-done | bytes 131104 | tf_op jit(solution)/shard_map/ppermute | solution.py:162
  4.6 6.4 %collective-permute-start.1 = (f32[16,2048]{1,0:T(8,128)S(1)}, f32[16,2048]{1,0:T(8,128)S(1)}, u32[]{:S(2)}, u32[]{:S(2)}) collective-permute-start(f32[16,2048]{1,0:T(8,128)S(1)} %shard_map.74.refs_0_), channel_id=1, source_target_pairs={{0,8},{1,9},{2,10},{3,11},{4,12},{5,13},{6,14},{7,15},{8,0},{9,1},... | collective-permute-start | bytes 393224 | tf_op jit(solution)/shard_map/ppermute | solution.py:162
  11.0 1.5 %collective-permute-start.6 = (f32[16,2048]{1,0:T(8,128)S(1)}, f32[16,2048]{1,0:T(8,128)S(1)}, u32[]{:S(2)}, u32[]{:S(2)}) collective-permute-start(f32[16,2048]{1,0:T(8,128)S(1)} %shard_map.74.refs_0_), channel_id=1, source_target_pairs={{0,2},{1,3},{2,0},{3,1},{4,6},{5,7},{6,4},{7,5},{8,10},{9,11},{10,... | collective-permute-start | bytes 393224 | tf_op jit(solution)/shard_map/ppermute | solution.py:162
  12.5 2.7 %collective-permute-start.7 = (f32[16,2048]{1,0:T(8,128)S(1)}, f32[16,2048]{1,0:T(8,128)S(1)}, u32[]{:S(2)}, u32[]{:S(2)}) collective-permute-start(f32[16,2048]{1,0:T(8,128)S(1)} %shard_map.74.refs_0_), channel_id=1, source_target_pairs={{0,4},{1,5},{2,6},{3,7},{4,0},{5,1},{6,2},{7,3},{8,12},{9,13},{10,... | collective-permute-start | bytes 393224 | tf_op jit(solution)/shard_map/ppermute | solution.py:162
  15.2 0.5 collective-permute-start.8
  15.7 2.0 %collective-permute-done.1.refs_0_ = f32[16,2048]{1,0:T(8,128)S(1)} collective-permute-done((f32[16,2048]{1,0:T(8,128)S(1)}, f32[16,2048]{1,0:T(8,128)S(1)}, u32[]{:S(2)}, u32[]{:S(2)}) %collective-permute-start.1) | collective-permute-done | bytes 131104 | tf_op jit(solution)/shard_map/ppermute | solution.py:162
  17.6 1.5 %collective-permute-start.2 = (f32[16,2048]{1,0:T(8,128)S(1)}, f32[16,2048]{1,0:T(8,128)S(1)}, u32[]{:S(2)}, u32[]{:S(2)}) collective-permute-start(f32[16,2048]{1,0:T(8,128)S(1)} %collective-permute-done.1.refs_0_), channel_id=1, source_target_pairs={{0,2},{1,3},{2,0},{3,1},{4,6},{5,7},{6,4},{7,5},{8,10},{9,11},{10,... | collective-permute-start | bytes 393224 | tf_op jit(solution)/shard_map/ppermute | solution.py:162
  19.1 0.0 collective-permute-done.6.refs_1_
  19.1 2.7 %collective-permute-start.3 = (f32[16,2048]{1,0:T(8,128)S(1)}, f32[16,2048]{1,0:T(8,128)S(1)}, u32[]{:S(2)}, u32[]{:S(2)}) collective-permute-start(f32[16,2048]{1,0:T(8,128)S(1)} %collective-permute-done.1.refs_0_), channel_id=1, source_target_pairs={{0,4},{1,5},{2,6},{3,7},{4,0},{5,1},{6,2},{7,3},{8,12},{9,13},{10,... | collective-permute-start | bytes 393224 | tf_op jit(solution)/shard_map/ppermute | solution.py:162
  21.9 0.0 collective-permute-done.5.other_ref
  21.9 0.5 collective-permute-start.4
  22.3 2.0 %shard_map.75 = (f32[32,128]{1,0:T(8,128)S(1)}, bf16[2048,512]{1,0:T(8,128)(2,1)S(1)}, bf16[2048,512]{1,0:T(8,128)(2,1)S(1)}) custom-call(f32[4,128]{1,0:T(4,128)} %bitcast.11, s32[2,4096]{1,0:T(2,128)} %bitcast.10, f32[64]{0:T(128)} %occ_ref.1, s32[2,256]{1,0:T(2,128)} %bitcast.12, f32[2048,256]{1,0:T(8,128)} %b_ref.1, ...), custom_call_target="tpu_custom_call" | custom-call | tf_op jit(solution)/shard_map/pallas_call | solution.py:186
  24.4 0.0 collective-permute-done.7.refs_2_
  24.4 0.0 collective-permute-done.8.refs_3_
  24.4 0.8 %shard_map.76.refs_6_ = f32[64,512]{1,0:T(8,128)S(1)} custom-call(f32[16,2048]{1,0:T(8,128)S(1)} %shard_map.74.refs_0_, f32[16,2048]{1,0:T(8,128)S(1)} %collective-permute-done.6.refs_1_, f32[16,2048]{1,0:T(8,128)S(1)} %collective-permute-done.7.refs_2_, f32[16,2048]{1,0:T(8,128)S(1)} %collective-permute-done.8.refs_3_, ...), custom_call_target="tpu_custom_call" | custom-call | tf_op jit(solution)/shard_map/pallas_call | solution.py:218
  25.1 0.0 copy-start
  25.2 0.0 collective-permute-done.2.refs_1_
  25.2 2.4 %collective-permute-done.3.refs_2_ = f32[16,2048]{1,0:T(8,128)S(1)} collective-permute-done((f32[16,2048]{1,0:T(8,128)S(1)}, f32[16,2048]{1,0:T(8,128)S(1)}, u32[]{:S(2)}, u32[]{:S(2)}) %collective-permute-start.3) | collective-permute-done | bytes 131104 | tf_op jit(solution)/shard_map/ppermute | solution.py:162
  27.5 2.0 %collective-permute-done.4.refs_3_ = f32[16,2048]{1,0:T(8,128)S(1)} collective-permute-done((f32[16,2048]{1,0:T(8,128)S(1)}, f32[16,2048]{1,0:T(8,128)S(1)}, u32[]{:S(2)}, u32[]{:S(2)}) %collective-permute-start.4) | collective-permute-done | bytes 131104 | tf_op jit(solution)/shard_map/ppermute | solution.py:162
  29.6 0.8 %shard_map.77 = f32[512,128]{1,0:T(8,128)S(1)} custom-call(f32[16,2048]{1,0:T(8,128)S(1)} %collective-permute-done.1.refs_0_, f32[16,2048]{1,0:T(8,128)S(1)} %collective-permute-done.2.refs_1_, f32[16,2048]{1,0:T(8,128)S(1)} %collective-permute-done.3.refs_2_, f32[16,2048]{1,0:T(8,128)S(1)} %collective-permute-done.4.refs_3_, ...), custom_call_target="tpu_custom_call" | custom-call | tf_op jit(solution)/shard_map/pallas_call | solution.py:229
  30.3 24.4 %all_to_all.5 = f32[128,1,512]{2,1,0:T(1,128)S(1)} all-to-all(f32[128,1,512]{2,1,0:T(1,128)S(1)} %bitcast.7), channel_id=1, replica_groups={{0,2,4,6,8,10,12,14,16,18,20,22,24,26,28,30,32,34,36,38,40,42,44,46,48,..., dimensions={0} | all-to-all | bytes 524288 | tf_op jit(solution)/shard_map/all_to_all | solution.py:237
  54.7 0.0 copy-done
  54.7 0.8 %shard_map.78 = f32[32,128]{1,0:T(8,128)} custom-call(f32[512,128]{1,0:T(8,128)S(1)} %bitcast.8, s32[32,128]{1,0:T(8,128)S(1)} %bitcast.9, f32[32,128]{1,0:T(8,128)S(1)} %get-tuple-element.10.denom_ref), custom_call_target="tpu_custom_call" | custom-call | tf_op jit(solution)/shard_map/pallas_call | solution.py:245
  (1 shorter events, 0.0 us)
Async XLA Ops:
  0.0 21.9 %collective-permute-start.5 = (f32[2048,256]{1,0:T(8,128)}, f32[2048,256]{1,0:T(8,128)S(1)}, u32[]{:S(2)}, u32[]{:S(2)}) collective-permute-start(f32[2048,256]{1,0:T(8,128)} %b_ref.1), channel_id=1, source_target_pairs={{0,1},{1,0},{2,3},{3,2},{4,5},{5,4},{6,7},{7,6},{8,9},{9,8},{10,11... | collective-permute-start | bytes 6291464 | tf_op jit(solution)/shard_map/ppermute | solution.py:162
  0.0 4.6 %collective-permute-start = (f32[16,2048]{1,0:T(8,128)}, f32[16,2048]{1,0:T(8,128)S(1)}, u32[]{:S(2)}, u32[]{:S(2)}) collective-permute-start(f32[16,2048]{1,0:T(8,128)} %block_ref.1), channel_id=1, source_target_pairs={{0,1},{1,0},{2,3},{3,2},{4,5},{5,4},{6,7},{7,6},{8,9},{9,8},{10,11... | collective-permute-start | bytes 393224 | tf_op jit(solution)/shard_map/ppermute | solution.py:162
  4.6 13.0 %collective-permute-start.1 = (f32[16,2048]{1,0:T(8,128)S(1)}, f32[16,2048]{1,0:T(8,128)S(1)}, u32[]{:S(2)}, u32[]{:S(2)}) collective-permute-start(f32[16,2048]{1,0:T(8,128)S(1)} %shard_map.74.refs_0_), channel_id=1, source_target_pairs={{0,8},{1,9},{2,10},{3,11},{4,12},{5,13},{6,14},{7,15},{8,0},{9,1},... | collective-permute-start | bytes 393224 | tf_op jit(solution)/shard_map/ppermute | solution.py:162
  11.0 8.1 %collective-permute-start.6 = (f32[16,2048]{1,0:T(8,128)S(1)}, f32[16,2048]{1,0:T(8,128)S(1)}, u32[]{:S(2)}, u32[]{:S(2)}) collective-permute-start(f32[16,2048]{1,0:T(8,128)S(1)} %shard_map.74.refs_0_), channel_id=1, source_target_pairs={{0,2},{1,3},{2,0},{3,1},{4,6},{5,7},{6,4},{7,5},{8,10},{9,11},{10,... | collective-permute-start | bytes 393224 | tf_op jit(solution)/shard_map/ppermute | solution.py:162
  12.5 11.9 %collective-permute-start.7 = (f32[16,2048]{1,0:T(8,128)S(1)}, f32[16,2048]{1,0:T(8,128)S(1)}, u32[]{:S(2)}, u32[]{:S(2)}) collective-permute-start(f32[16,2048]{1,0:T(8,128)S(1)} %shard_map.74.refs_0_), channel_id=1, source_target_pairs={{0,4},{1,5},{2,6},{3,7},{4,0},{5,1},{6,2},{7,3},{8,12},{9,13},{10,... | collective-permute-start | bytes 393224 | tf_op jit(solution)/shard_map/ppermute | solution.py:162
  15.2 9.2 %collective-permute-start.8 = (f32[16,2048]{1,0:T(8,128)S(1)}, f32[16,2048]{1,0:T(8,128)S(1)}, u32[]{:S(2)}, u32[]{:S(2)}) collective-permute-start(f32[16,2048]{1,0:T(8,128)S(1)} %shard_map.74.refs_0_), channel_id=1, source_target_pairs={{0,6},{1,7},{2,4},{3,5},{4,2},{5,3},{6,0},{7,1},{8,14},{9,15},{10,... | collective-permute-start | bytes 393224 | tf_op jit(solution)/shard_map/ppermute | solution.py:162
  17.6 7.5 %collective-permute-start.2 = (f32[16,2048]{1,0:T(8,128)S(1)}, f32[16,2048]{1,0:T(8,128)S(1)}, u32[]{:S(2)}, u32[]{:S(2)}) collective-permute-start(f32[16,2048]{1,0:T(8,128)S(1)} %collective-permute-done.1.refs_0_), channel_id=1, source_target_pairs={{0,2},{1,3},{2,0},{3,1},{4,6},{5,7},{6,4},{7,5},{8,10},{9,11},{10,... | collective-permute-start | bytes 393224 | tf_op jit(solution)/shard_map/ppermute | solution.py:162
  19.1 8.4 %collective-permute-start.3 = (f32[16,2048]{1,0:T(8,128)S(1)}, f32[16,2048]{1,0:T(8,128)S(1)}, u32[]{:S(2)}, u32[]{:S(2)}) collective-permute-start(f32[16,2048]{1,0:T(8,128)S(1)} %collective-permute-done.1.refs_0_), channel_id=1, source_target_pairs={{0,4},{1,5},{2,6},{3,7},{4,0},{5,1},{6,2},{7,3},{8,12},{9,13},{10,... | collective-permute-start | bytes 393224 | tf_op jit(solution)/shard_map/ppermute | solution.py:162
  21.9 7.7 %collective-permute-start.4 = (f32[16,2048]{1,0:T(8,128)S(1)}, f32[16,2048]{1,0:T(8,128)S(1)}, u32[]{:S(2)}, u32[]{:S(2)}) collective-permute-start(f32[16,2048]{1,0:T(8,128)S(1)} %collective-permute-done.1.refs_0_), channel_id=1, source_target_pairs={{0,6},{1,7},{2,4},{3,5},{4,2},{5,3},{6,0},{7,1},{8,14},{9,15},{10,... | collective-permute-start | bytes 393224 | tf_op jit(solution)/shard_map/ppermute | solution.py:162
  25.1 29.6 %copy-start = (s32[4096]{0:T(1024)S(1)}, s32[4096]{0:T(1024)}, u32[]{:S(2)}) copy-start(s32[4096]{0:T(1024)} %param.9) | copy-start | bytes 49156
